TPU v7x, 32 devices: a whole 2x2x4 slice. The times are simulated.
32 devices in a mesh: blk: 16 (over z, x, core), head: 2 (over y).
Axes of the slice: x: 2, y: 2, z: 4, core: 2. Of those that a mesh axis runs over, the one named last changes fastest.
Arguments:
- query: bfloat16 [4096, 4096], P(('blk', 'head')), may hold values from -128 to 128
- key: bfloat16 [2048, 4096], P('blk', 'head'), may hold values from -8 to 8
- value: bfloat16 [2048, 4096], P('blk', 'head'), may hold values from -6 to 6
- d_out: bfloat16 [4096, 4096], P(('blk', 'head')), may hold values from -6 to 6
- seg_map: int32 [32], replicated, may hold values from 0 to 7, never falling along the last dimension, each value on 1 to 8 neighbouring positions
- spans: int32 [8, 8], replicated, may hold values from 0 to 15, all different within a row
Outputs:
- attn_out: bfloat16 [4096, 4096], P(('blk', 'head'))
- d_query: bfloat16 [4096, 4096], P(('blk', 'head'))
- d_key: bfloat16 [2048, 4096], P('blk', 'head')
- d_value: bfloat16 [2048, 4096], P('blk', 'head')
Inputs may be any that keep to these rules, and one draw needn't show every extreme that they name: `seg_map`: segment numbers never fall from one CAD block to the next; each segment covers 1 to 8 blocks, one exactly 8. `spans`: each row names 8 different document blocks; every document block is named by some row.
All inputs are finite; a program needn't handle non-finite values.
Results may differ from a plain program's by a relative error of at most 0.024.
Values may be sent and summed in bfloat16 or wider, within the bound.
A program may use at most 128 MiB of HBM per device.

v0:
```python
import math

import jax
import jax.numpy as jnp
from jax import lax
from jax.sharding import PartitionSpec as P

HEADS = 32
HEAD_DIM = 128
BLOCK = 128
SPANS = 8


def head_pass(q_head, dout_head, key_head, value_head, id_groups):
    factor = 1.0 / math.sqrt(HEAD_DIM)
    group_width = q_head.shape[1]
    doc_blocks = key_head.shape[0]

    def one_group(sums, inputs):
        q_group, dout_group, group_ids = inputs
        flat_ids = group_ids.reshape(group_width * SPANS)
        key_tiles = jnp.take(key_head, flat_ids, axis=0).reshape(
            group_width, SPANS * BLOCK, HEAD_DIM
        )
        value_tiles = jnp.take(value_head, flat_ids, axis=0).reshape(
            group_width, SPANS * BLOCK, HEAD_DIM
        )
        scores = (
            jnp.einsum("cqd,ckd->cqk", q_group, key_tiles, preferred_element_type=jnp.float32)
            * factor
        )
        top_score = jnp.max(scores, axis=-1, keepdims=True)
        expo = jnp.exp(scores - top_score)
        prob = expo / jnp.sum(expo, axis=-1, keepdims=True)
        prob_b = prob.astype(jnp.bfloat16)
        attn = jnp.einsum("cqk,ckd->cqd", prob_b, value_tiles, preferred_element_type=jnp.float32)
        delta = jnp.sum(dout_group.astype(jnp.float32) * attn, axis=-1, keepdims=True)
        dprob = jnp.einsum(
            "cqd,ckd->cqk", dout_group, value_tiles, preferred_element_type=jnp.float32
        )
        dscore_b = (prob * (dprob - delta)).astype(jnp.bfloat16)
        grad_query = (
            jnp.einsum("cqk,ckd->cqd", dscore_b, key_tiles, preferred_element_type=jnp.float32)
            * factor
        ).astype(jnp.bfloat16)
        key_slots = (
            jnp.einsum("cqk,cqd->ckd", dscore_b, q_group, preferred_element_type=jnp.float32)
            * factor
        )
        value_slots = jnp.einsum(
            "cqk,cqd->ckd", prob_b, dout_group, preferred_element_type=jnp.float32
        )
        one_hot = (jnp.arange(doc_blocks, dtype=jnp.int32)[:, None] == flat_ids[None, :]).astype(
            jnp.float32
        )
        key_sums = sums[0] + jnp.dot(
            one_hot,
            key_slots.reshape(group_width * SPANS, BLOCK * HEAD_DIM),
            precision=lax.Precision.HIGHEST,
            preferred_element_type=jnp.float32,
        )
        value_sums = sums[1] + jnp.dot(
            one_hot,
            value_slots.reshape(group_width * SPANS, BLOCK * HEAD_DIM),
            precision=lax.Precision.HIGHEST,
            preferred_element_type=jnp.float32,
        )
        return ((key_sums, value_sums), (attn.astype(jnp.bfloat16), grad_query))

    zero_sums = jnp.zeros((doc_blocks, BLOCK * HEAD_DIM), jnp.float32)
    (key_sums, value_sums), (attn_head, grad_head) = lax.scan(
        one_group, (zero_sums, zero_sums), (q_head, dout_head, id_groups)
    )
    return (attn_head, grad_head, key_sums, value_sums)


def block_table(global_blocks, seg_map, spans):
    block_count = global_blocks.shape[0]
    seg_match = (
        global_blocks[:, None] == jnp.arange(seg_map.shape[0], dtype=jnp.int32)[None, :]
    ).astype(jnp.int32)
    seg_here = jnp.sum(seg_match * seg_map[None, :], axis=1)
    span_match = (seg_here[:, None] == jnp.arange(spans.shape[0], dtype=jnp.int32)[None, :]).astype(
        jnp.int32
    )
    block_ids = jnp.sum(span_match[:, :, None] * spans[None, :, :], axis=1)
    group_width = math.gcd(block_count, max(1, 512 // BLOCK))
    group_count = block_count // group_width
    return (block_ids.reshape(group_count, group_width, SPANS), group_count, group_width)


def by_heads(array, heads_count, group_count, group_width):
    block_count = group_count * group_width
    shaped = array.reshape(block_count, BLOCK, heads_count, HEAD_DIM).transpose(2, 0, 1, 3)
    return shaped.reshape(heads_count, group_count, group_width, BLOCK, HEAD_DIM)


def from_heads(array, heads_count):
    row_count = array.shape[1] * array.shape[2] * BLOCK
    shaped = array.reshape(heads_count, row_count, HEAD_DIM).transpose(1, 0, 2)
    return shaped.reshape(row_count, heads_count * HEAD_DIM)


def from_head_sums(array, heads_count):
    doc_rows = array.shape[1] // HEAD_DIM * BLOCK // BLOCK * array.shape[0] // array.shape[0]
    doc_rows = array.shape[1] * array.shape[2] // (BLOCK * HEAD_DIM) * BLOCK
    shaped = array.reshape(heads_count, doc_rows, HEAD_DIM).transpose(1, 0, 2)
    return shaped.reshape(doc_rows, heads_count * HEAD_DIM)


def body(query, key, value, d_out, seg_map, spans):
    dummy_carry = jnp.zeros((), jnp.int32)
    heads_here = HEADS // lax.axis_size("blk")
    q_rows, dout_rows = (
        lax.all_to_all(query, "blk", split_axis=1, concat_axis=0, tiled=True),
        lax.all_to_all(d_out, "blk", split_axis=1, concat_axis=0, tiled=True),
    )
    per_device = query.shape[0] // BLOCK
    block_count = q_rows.shape[0] // BLOCK
    local_blocks = jnp.arange(block_count, dtype=jnp.int32)
    global_blocks = (
        local_blocks // per_device * lax.axis_size("head") + lax.axis_index("head")
    ) * per_device + local_blocks % per_device
    id_groups, group_count, group_width = block_table(global_blocks, seg_map, spans)
    q_heads = by_heads(q_rows, heads_here, group_count, group_width)
    dout_heads = by_heads(dout_rows, heads_here, group_count, group_width)
    key_wide, value_wide = (
        lax.all_gather(key, "head", axis=1, tiled=True),
        lax.all_gather(value, "head", axis=1, tiled=True),
    )
    key_cols, value_cols = (
        lax.all_to_all(key_wide, "blk", split_axis=1, concat_axis=0, tiled=True),
        lax.all_to_all(value_wide, "blk", split_axis=1, concat_axis=0, tiled=True),
    )
    doc_blocks = key_cols.shape[0] // BLOCK

    def to_blocks(array):
        return array.reshape(doc_blocks, BLOCK, heads_here, HEAD_DIM).transpose(2, 0, 1, 3)

    def scan_head(carry, inputs):
        q_head, dout_head, key_head, value_head = inputs
        return (carry, head_pass(q_head, dout_head, key_head, value_head, id_groups))

    _, (attn_heads, grad_heads, key_parts, value_parts) = lax.scan(
        scan_head, dummy_carry, (q_heads, dout_heads, to_blocks(key_cols), to_blocks(value_cols))
    )
    key_back, value_back = (
        lax.all_to_all(
            from_head_sums(key_parts, heads_here).astype(jnp.bfloat16),
            "blk",
            split_axis=0,
            concat_axis=1,
            tiled=True,
        ).astype(jnp.float32),
        lax.all_to_all(
            from_head_sums(value_parts, heads_here).astype(jnp.bfloat16),
            "blk",
            split_axis=0,
            concat_axis=1,
            tiled=True,
        ).astype(jnp.float32),
    )
    key_total, value_total = (
        lax.psum_scatter(
            key_back.astype(jnp.bfloat16), "head", scatter_dimension=1, tiled=True
        ).astype(jnp.float32),
        lax.psum_scatter(
            value_back.astype(jnp.bfloat16), "head", scatter_dimension=1, tiled=True
        ).astype(jnp.float32),
    )
    attn_out, d_query = (
        lax.all_to_all(
            from_heads(attn_heads, heads_here), "blk", split_axis=0, concat_axis=1, tiled=True
        ),
        lax.all_to_all(
            from_heads(grad_heads, heads_here), "blk", split_axis=0, concat_axis=1, tiled=True
        ),
    )
    return (attn_out, d_query, key_total.astype(jnp.bfloat16), value_total.astype(jnp.bfloat16))


def solution(mesh):
    placed = (
        P(("blk", "head"), None),
        P("blk", "head"),
        P("blk", "head"),
        P(("blk", "head"), None),
        P(),
        P(),
    )
    return jax.shard_map(
        body,
        mesh=mesh,
        in_specs=placed,
        out_specs=(
            P(("blk", "head"), None),
            P(("blk", "head"), None),
            P("blk", "head"),
            P("blk", "head"),
        ),
        check_vma=False,
    )
```

profile of v0, /device:TPU:0, one launch (start us, length us, event | category | flops | bytes accessed | tf_op | source)
XLA Modules:
  0.0 560.5 jit_solution(10621087796249893933)
XLA Ops:
  7.2 2.4 copy.94
  9.5 7.4 %all-to-all-start = ((bf16[128,16,256]{0,2,1:T(8,128)(2,1)}), bf16[128,16,256]{0,2,1:T(8,128)(2,1)}, u32[]{:S(2)}, u32[]{:S(2)}) async-start(bf16[128,16,256]{0,2,1:T(8,128)(2,1)} %bitcast.8), calls=%async_computation | async-start | bytes 2097152 | tf_op jit(solution)/shard_map/all_to_all | solution.py:115
  18.3 21.6 %all-to-all-done = bf16[128,16,256]{0,2,1:T(8,128)(2,1)} async-done(((bf16[128,16,256]{0,2,1:T(8,128)(2,1)}), bf16[128,16,256]{0,2,1:T(8,128)(2,1)}, u32[]{:S(2)}, u32[]{:S(2)}) %all-to-all-start) | async-done | bytes 1048608 | tf_op jit(solution)/shard_map/all_to_all | solution.py:115
  39.9 6.8 %all-to-all-start.1 = ((bf16[128,16,256]{0,2,1:T(8,128)(2,1)}), bf16[128,16,256]{0,2,1:T(8,128)(2,1)}, u32[]{:S(2)}, u32[]{:S(2)}) async-start(bf16[128,16,256]{0,2,1:T(8,128)(2,1)} %bitcast.13), calls=%async_computation.1 | async-start | bytes 2097152 | tf_op jit(solution)/shard_map/all_to_all | solution.py:116
  47.5 24.2 %all-gather.5.cloned.1.call-done = bf16[128,4096]{1,0:T(8,128)(2,1)} async-done(((bf16[128,2048]{1,0:T(8,128)(2,1)}), bf16[128,4096]{1,0:T(8,128)(2,1)}) %all-gather.5.cloned.1.call-update) | async-done | bytes 1048592 | tf_op jit(solution)/shard_map/all_gather | solution.py:129
  71.7 2.3 copy.97
  74.0 5.7 %all-to-all-start.3 = ((bf16[128,16,256]{0,2,1:T(8,128)(2,1)}), bf16[128,16,256]{0,2,1:T(8,128)(2,1)}, u32[]{:S(2)}, u32[]{:S(2)}) async-start(bf16[128,16,256]{0,2,1:T(8,128)(2,1)} %bitcast.22), calls=%async_computation.3 | async-start | bytes 2097152 | tf_op jit(solution)/shard_map/all_to_all | solution.py:133
  80.4 23.2 %all-gather.3.cloned.1.call-done = bf16[128,4096]{1,0:T(8,128)(2,1)} async-done(((bf16[128,2048]{1,0:T(8,128)(2,1)}), bf16[128,4096]{1,0:T(8,128)(2,1)}) %all-gather.3.cloned.1.call-update) | async-done | bytes 1048592 | tf_op jit(solution)/shard_map/all_gather | solution.py:128
  103.7 2.3 copy.96
  106.0 5.7 %all-to-all-start.2 = ((bf16[128,16,256]{0,2,1:T(8,128)(2,1)}), bf16[128,16,256]{0,2,1:T(8,128)(2,1)}, u32[]{:S(2)}, u32[]{:S(2)}) async-start(bf16[128,16,256]{0,2,1:T(8,128)(2,1)} %bitcast.18), calls=%async_computation.2 | async-start | bytes 2097152 | tf_op jit(solution)/shard_map/all_to_all | solution.py:132
  112.1 22.5 %all-to-all-done.2 = bf16[128,16,256]{0,2,1:T(8,128)(2,1)} async-done(((bf16[128,16,256]{0,2,1:T(8,128)(2,1)}), bf16[128,16,256]{0,2,1:T(8,128)(2,1)}, u32[]{:S(2)}, u32[]{:S(2)}) %all-to-all-start.2) | async-done | bytes 1048608 | tf_op jit(solution)/shard_map/all_to_all | solution.py:132
  134.6 291.7 %while.34 = (s32[]{:T(128)}, bf16[2,4,4,128,128]{4,3,2,1,0:T(8,128)(2,1)}, bf16[2,4,4,128,128]{4,3,2,1,0:T(8,128)(2,1)}, bf16[2,16,16384]{2,1,0:T(8,128)(2,1)}, ...) while((s32[]{:T(128)}, ...), condition=%wide.region_8.10_spmd, body=%wide.region_2.9_spmd.sunk | while | flops 1014369024 | bytes 101597424 | solution.py:144
  143.0 131.8 %while.35 = (s32[]{:T(128)}, f32[16,16384]{1,0:T(8,128)}, f32[16,16384]{1,0:T(8,128)}, bf16[4,4,128,128]{2,3,1,0:T(8,128)(2,1)}, bf16[4,4,128,128]{3,2,1,0:T(8,1...) while((s32[]{:T(128)}, f32[16,16384]{1,0:T(8,128)}, ...), condition=%wide.region_7.8_spmd.clone, body=%wide.region_3.7_spmd.clone.sunk | while | flops 1014369024 | bytes 69091184 | solution.py:71
  148.0 3.0 fusion.78
  159.6 2.8 convolution_multiply_fusion.3
  162.4 2.9 reshape.176
  165.2 2.8 convolution_add_fusion.4
  169.1 2.8 fusion.80
  180.9 3.0 fusion.78
  192.6 2.8 convolution_multiply_fusion.3
  195.3 2.9 reshape.176
  198.2 2.8 convolution_add_fusion.4
  202.0 2.8 fusion.80
  213.9 3.0 fusion.78
  225.5 2.8 convolution_multiply_fusion.3
  228.3 2.9 reshape.176
  231.1 2.8 convolution_add_fusion.4
  234.9 2.8 fusion.80
  246.8 3.0 fusion.78
  258.4 2.8 convolution_multiply_fusion.3
  261.2 2.9 reshape.176
  264.1 2.8 convolution_add_fusion.4
  267.9 2.8 fusion.80
  276.3 2.2 bitcast_dynamic-update-slice_fusion.7
  288.9 131.8 %while.35 = (s32[]{:T(128)}, f32[16,16384]{1,0:T(8,128)}, f32[16,16384]{1,0:T(8,128)}, bf16[4,4,128,128]{2,3,1,0:T(8,128)(2,1)}, bf16[4,4,128,128]{3,2,1,0:T(8,1...) while((s32[]{:T(128)}, f32[16,16384]{1,0:T(8,128)}, ...), condition=%wide.region_7.8_spmd.clone, body=%wide.region_3.7_spmd.clone.sunk | while | flops 1014369024 | bytes 69091184 | solution.py:71
  293.9 3.0 fusion.78
  305.5 2.8 convolution_multiply_fusion.3
  308.3 2.9 reshape.176
  311.1 2.8 convolution_add_fusion.4
  314.9 2.8 fusion.80
  326.8 3.0 fusion.78
  338.4 2.8 convolution_multiply_fusion.3
  341.2 2.9 reshape.176
  344.0 2.8 convolution_add_fusion.4
  347.9 2.8 fusion.80
  359.7 3.0 fusion.78
  371.4 2.8 convolution_multiply_fusion.3
  374.1 2.9 reshape.176
  377.0 2.8 convolution_add_fusion.4
  380.8 2.8 fusion.80
  392.7 3.0 fusion.78
  404.3 2.8 convolution_multiply_fusion.3
  407.1 2.9 reshape.176
  409.9 2.8 convolution_add_fusion.4
  413.7 2.8 fusion.80
  422.1 2.2 bitcast_dynamic-update-slice_fusion.7
  429.8 6.8 %all-to-all-start.7 = ((bf16[16,128,256]{1,2,0:T(8,128)(2,1)}), bf16[16,128,256]{1,2,0:T(8,128)(2,1)S(1)}, u32[]{:S(2)}, u32[]{:S(2)}) async-start(bf16[16,128,256]{1,2,0:T(8,128)(2,1)} %copy.112), calls=%async_computation.8 | async-start | bytes 2097152 | tf_op jit(solution)/shard_map/all_to_all | solution.py:155
  439.2 20.3 %all-to-all-done.7 = bf16[16,128,256]{1,2,0:T(8,128)(2,1)S(1)} async-done(((bf16[16,128,256]{1,2,0:T(8,128)(2,1)}), bf16[16,128,256]{1,2,0:T(8,128)(2,1)S(1)}, u32[]{:S(2)}, u32[]{:S(2)}) %all-to-all-start.7) | async-done | bytes 1048608 | tf_op jit(solution)/shard_map/all_to_all | solution.py:155
  459.5 6.8 %all-to-all-start.6 = ((bf16[16,128,256]{1,2,0:T(8,128)(2,1)}), bf16[16,128,256]{1,2,0:T(8,128)(2,1)S(1)}, u32[]{:S(2)}, u32[]{:S(2)}) async-start(bf16[16,128,256]{1,2,0:T(8,128)(2,1)} %copy.110), calls=%async_computation.6 | async-start | bytes 2097152 | tf_op jit(solution)/shard_map/all_to_all | solution.py:148
  469.1 20.1 %all-to-all-done.6 = bf16[16,128,256]{1,2,0:T(8,128)(2,1)S(1)} async-done(((bf16[16,128,256]{1,2,0:T(8,128)(2,1)}), bf16[16,128,256]{1,2,0:T(8,128)(2,1)S(1)}, u32[]{:S(2)}, u32[]{:S(2)}) %all-to-all-start.6) | async-done | bytes 1048608 | tf_op jit(solution)/shard_map/all_to_all | solution.py:148
  489.2 6.8 %all-to-all-start.4 = ((bf16[16,128,256]{1,2,0:T(8,128)(2,1)}), bf16[16,128,256]{1,2,0:T(8,128)(2,1)S(1)}, u32[]{:S(2)}, u32[]{:S(2)}) async-start(bf16[16,128,256]{1,2,0:T(8,128)(2,1)} %copy.106), calls=%async_computation.4 | async-start | bytes 2097152 | tf_op jit(solution)/shard_map/all_to_all | solution.py:172
  498.7 20.3 %all-to-all-done.4 = bf16[16,128,256]{1,2,0:T(8,128)(2,1)S(1)} async-done(((bf16[16,128,256]{1,2,0:T(8,128)(2,1)}), bf16[16,128,256]{1,2,0:T(8,128)(2,1)S(1)}, u32[]{:S(2)}, u32[]{:S(2)}) %all-to-all-start.4) | async-done | bytes 1048608 | tf_op jit(solution)/shard_map/all_to_all | solution.py:172
  518.9 6.8 %all-to-all-start.5 = ((bf16[16,128,256]{1,2,0:T(8,128)(2,1)}), bf16[16,128,256]{1,2,0:T(8,128)(2,1)S(1)}, u32[]{:S(2)}, u32[]{:S(2)}) async-start(bf16[16,128,256]{1,2,0:T(8,128)(2,1)} %copy.108), calls=%async_computation.5 | async-start | bytes 2097152 | tf_op jit(solution)/shard_map/all_to_all | solution.py:175
  527.0 21.6 %all-to-all-done.5 = bf16[16,128,256]{1,2,0:T(8,128)(2,1)S(1)} async-done(((bf16[16,128,256]{1,2,0:T(8,128)(2,1)}), bf16[16,128,256]{1,2,0:T(8,128)(2,1)S(1)}, u32[]{:S(2)}, u32[]{:S(2)}) %all-to-all-start.5) | async-done | bytes 1048608 | tf_op jit(solution)/shard_map/all_to_all | solution.py:175
  (308 shorter events, 193.7 us)
Async XLA Ops:
  7.2 9.8 %copy-start.9 = (bf16[128,4096]{1,0:T(8,128)(2,1)S(1)}, bf16[128,4096]{1,0:T(8,128)(2,1)}, u32[]{:S(2)}) copy-start(bf16[128,4096]{1,0:T(8,128)(2,1)} %param.15) | copy-start | bytes 3145732
  9.5 30.4 %all-to-all-start = ((bf16[128,16,256]{0,2,1:T(8,128)(2,1)}), bf16[128,16,256]{0,2,1:T(8,128)(2,1)}, u32[]{:S(2)}, u32[]{:S(2)}) async-start(bf16[128,16,256]{0,2,1:T(8,128)(2,1)} %bitcast.8), calls=%async_computation | async-start | bytes 2097152 | tf_op jit(solution)/shard_map/all_to_all | solution.py:115
  39.9 34.1 %all-to-all-start.1 = ((bf16[128,16,256]{0,2,1:T(8,128)(2,1)}), bf16[128,16,256]{0,2,1:T(8,128)(2,1)}, u32[]{:S(2)}, u32[]{:S(2)}) async-start(bf16[128,16,256]{0,2,1:T(8,128)(2,1)} %bitcast.13), calls=%async_computation.1 | async-start | bytes 2097152 | tf_op jit(solution)/shard_map/all_to_all | solution.py:116
  46.8 25.0 %all-gather.5.cloned.1.call-start = ((), (), s32[]{:S(2)}) async-start(), calls=%async_computation.11 | async-start | bytes 1572864 | tf_op jit(solution)/shard_map/all_gather | solution.py:129
  74.0 32.0 %all-to-all-start.3 = ((bf16[128,16,256]{0,2,1:T(8,128)(2,1)}), bf16[128,16,256]{0,2,1:T(8,128)(2,1)}, u32[]{:S(2)}, u32[]{:S(2)}) async-start(bf16[128,16,256]{0,2,1:T(8,128)(2,1)} %bitcast.22), calls=%async_computation.3 | async-start | bytes 2097152 | tf_op jit(solution)/shard_map/all_to_all | solution.py:133
  79.7 24.0 %all-gather.3.cloned.1.call-start = ((), (), s32[]{:S(2)}) async-start(), calls=%async_computation.10 | async-start | bytes 1572864 | tf_op jit(solution)/shard_map/all_gather | solution.py:128
  80.4 31.3 %copy-start.16 = (s32[32]{0:T(128)S(1)}, s32[32]{0:T(128)}, u32[]{:S(2)}) copy-start(s32[32]{0:T(128)} %param.16) | copy-start | bytes 388
  80.4 31.5 %copy-start.15 = (s32[8,8]{1,0:T(8,128)S(1)}, s32[8,8]{1,0:T(8,128)}, u32[]{:S(2)}) copy-start(s32[8,8]{1,0:T(8,128)} %param.17) | copy-start | bytes 772
  106.0 28.6 %all-to-all-start.2 = ((bf16[128,16,256]{0,2,1:T(8,128)(2,1)}), bf16[128,16,256]{0,2,1:T(8,128)(2,1)}, u32[]{:S(2)}, u32[]{:S(2)}) async-start(bf16[128,16,256]{0,2,1:T(8,128)(2,1)} %bitcast.18), calls=%async_computation.2 | async-start | bytes 2097152 | tf_op jit(solution)/shard_map/all_to_all | solution.py:132
  151.0 2.0 copy-start
  162.4 2.9 copy-start.4
  168.1 1.0 copy-start.5
  171.8 1.9 copy-start.1
  175.0 1.0 copy-start.2
  183.9 2.0 copy-start
  195.3 2.9 copy-start.4
  201.0 1.0 copy-start.5
  204.8 1.9 copy-start.1
  207.9 1.0 copy-start.2
  216.9 2.0 copy-start
  228.3 2.9 copy-start.4
  234.0 1.0 copy-start.5
  237.7 1.9 copy-start.1
  240.8 1.0 copy-start.2
  249.8 2.0 copy-start
  261.2 2.9 copy-start.4
  266.9 1.0 copy-start.5
  270.7 1.9 copy-start.1
  273.8 1.0 copy-start.2
  274.8 3.7 copy-start.3
  274.8 3.7 copy-start.6
  276.3 2.2 copy-start.10
  279.4 1.0 copy-start.11
  296.9 2.0 copy-start
  308.3 2.9 copy-start.4
  317.7 1.9 copy-start.1
  320.8 1.0 copy-start.2
  329.8 2.0 copy-start
  341.2 2.9 copy-start.4
  350.6 1.9 copy-start.1
  353.8 1.0 copy-start.2
  362.7 2.0 copy-start
  374.1 2.9 copy-start.4
  383.6 1.9 copy-start.1
  386.7 1.0 copy-start.2
  395.7 2.0 copy-start
  407.1 2.9 copy-start.4
  416.5 1.9 copy-start.1
  419.7 1.0 copy-start.2
  420.7 3.7 copy-start.3
  420.7 3.7 copy-start.6
  422.1 2.2 copy-start.10
  425.2 1.0 copy-start.11
  428.6 8.1 %copy-start.12 = (bf16[2,16,16384]{2,1,0:T(8,128)(2,1)S(1)}, bf16[2,16,16384]{2,1,0:T(8,128)(2,1)}, u32[]{:S(2)}) copy-start(bf16[2,16,16384]{2,1,0:T(8,128)(2,1)} %get-tuple-element.117) | copy-start | bytes 3145732
  429.8 29.7 %all-to-all-start.7 = ((bf16[16,128,256]{1,2,0:T(8,128)(2,1)}), bf16[16,128,256]{1,2,0:T(8,128)(2,1)S(1)}, u32[]{:S(2)}, u32[]{:S(2)}) async-start(bf16[16,128,256]{1,2,0:T(8,128)(2,1)} %copy.112), calls=%async_computation.8 | async-start | bytes 2097152 | tf_op jit(solution)/shard_map/all_to_all | solution.py:155
  439.2 27.9 %copy-start.14 = (bf16[2,4,4,128,128]{4,3,2,1,0:T(8,128)(2,1)S(1)}, bf16[2,4,4,128,128]{4,3,2,1,0:T(8,128)(2,1)}, u32[]{:S(2)}) copy-start(bf16[2,4,4,128,128]{4,3,2,1,0:T(8,128)(2,1)} %get-tuple-element.115) | copy-start | bytes 3145732
  459.5 7.0 %copy-start.7 = (bf16[16,128,256]{1,2,0:T(8,128)(2,1)}, bf16[16,128,256]{1,2,0:T(8,128)(2,1)S(1)}, u32[]{:S(2)}) copy-start(bf16[16,128,256]{1,2,0:T(8,128)(2,1)S(1)} %all-to-all-done.7) | copy-start | bytes 3145732
  459.5 29.7 %all-to-all-start.6 = ((bf16[16,128,256]{1,2,0:T(8,128)(2,1)}), bf16[16,128,256]{1,2,0:T(8,128)(2,1)S(1)}, u32[]{:S(2)}, u32[]{:S(2)}) async-start(bf16[16,128,256]{1,2,0:T(8,128)(2,1)} %copy.110), calls=%async_computation.6 | async-start | bytes 2097152 | tf_op jit(solution)/shard_map/all_to_all | solution.py:148
  466.3 83.6 %reduce-scatter.5.cloned.1.call-start = ((), (), s32[]{:S(2)}) async-start(), calls=%async_computation.13 | async-start | bytes 1572864 | tf_op jit(solution)/shard_map/reduce_scatter | solution.py:167
  469.1 27.5 %copy-start.13 = (bf16[2,4,4,128,128]{4,3,2,1,0:T(8,128)(2,1)S(1)}, bf16[2,4,4,128,128]{4,3,2,1,0:T(8,128)(2,1)}, u32[]{:S(2)}) copy-start(bf16[2,4,4,128,128]{4,3,2,1,0:T(8,128)(2,1)} %get-tuple-element.116) | copy-start | bytes 3145732
  489.2 6.8 %copy-start.8 = (bf16[16,128,256]{1,2,0:T(8,128)(2,1)}, bf16[16,128,256]{1,2,0:T(8,128)(2,1)S(1)}, u32[]{:S(2)}) copy-start(bf16[16,128,256]{1,2,0:T(8,128)(2,1)S(1)} %all-to-all-done.6) | copy-start | bytes 3145732
  489.2 29.7 %all-to-all-start.4 = ((bf16[16,128,256]{1,2,0:T(8,128)(2,1)}), bf16[16,128,256]{1,2,0:T(8,128)(2,1)S(1)}, u32[]{:S(2)}, u32[]{:S(2)}) async-start(bf16[16,128,256]{1,2,0:T(8,128)(2,1)} %copy.106), calls=%async_computation.4 | async-start | bytes 2097152 | tf_op jit(solution)/shard_map/all_to_all | solution.py:172
  496.0 55.9 %reduce-scatter.3.cloned.1.call-start = ((), (), s32[]{:S(2)}) async-start(), calls=%async_computation.12 | async-start | bytes 1572864 | tf_op jit(solution)/shard_map/reduce_scatter | solution.py:164
  518.9 29.7 %all-to-all-start.5 = ((bf16[16,128,256]{1,2,0:T(8,128)(2,1)}), bf16[16,128,256]{1,2,0:T(8,128)(2,1)S(1)}, u32[]{:S(2)}, u32[]{:S(2)}) async-start(bf16[16,128,256]{1,2,0:T(8,128)(2,1)} %copy.108), calls=%async_computation.5 | async-start | bytes 2097152 | tf_op jit(solution)/shard_map/all_to_all | solution.py:175
  (4 other events, 3.9 us)
Sparse Core Ops, SparseCore 0:
  49.1 22.5 all-gather.4
  82.0 21.6 all-gather.2
  469.4 20.7 reduce-scatter.4
  498.8 20.7 reduce-scatter.2
where the time goes:
time: 565 us; the launch traced here: 561 us
  waiting for transfers between devices  176 us (31%)
  local copies, waits for them, and re-layouts  144 us (25%)
  matrix products  137 us (24%)
  starting transfers between devices  53.1 us (9%)
  other arithmetic  34.6 us (6%)
  between operations  14.1 us (2%)
    all_gather x1, waiting for transfers between devices, body(): lax.all_gather(value, 'head', axis=1, tiled=True)  24.2 us
    sub x8, matrix products, one_group(): expo = jnp.exp(scores - top_score)  24.1 us
    all_gather x1, waiting for transfers between devices, body(): lax.all_gather(key, 'head', axis=1, tiled=True)  23.2 us
    reshape x8, local copies, waits for them, and re-layouts, one_group(): key_slots.reshape(group_width * SPANS, BLOCK * HEAD_DIM)  22.8 us
    dot_general x8, matrix products, one_group(): jnp.dot(one_hot, key_slots.reshape(group_width * SPANS, BLOCK * HEAD_DIM)...  22.6 us
    all_to_all x1, waiting for transfers between devices, body(): lax.all_to_all(key_wide, 'blk', split_axis=1, concat_axis=0, tiled=True)  22.5 us
    dot_general x8, matrix products, one_group(): jnp.einsum('cqk,cqd->ckd', prob_b, dout_group, preferred_element_type=jnp...  22.3 us
    dot_general x8, matrix products, one_group(): jnp.einsum('cqk,cqd->ckd', dscore_b, q_group, preferred_element_type=jnp....  22.1 us
  transfers between devices with their start and end apart: 12, of which 8 were waited for; matrix products, arithmetic and copies ran while one was open for 3% of the time, Pallas kernels for 0%

commit v1 on v0

--- a/solution.py
+++ b/solution.py
@@ -1,15 +1,88 @@
+import functools
 import math
 
-import jax
-import jax.numpy as jnp
+import jax, jax.numpy as jnp
 from jax import lax
+from jax.experimental import pallas as pl
+from jax.experimental.pallas import tpu as pltpu
 from jax.sharding import PartitionSpec as P
+
 
 HEADS = 32
 HEAD_DIM = 128
 BLOCK = 128
 SPANS = 8
-
+NT = (((1,), (1,)), ((), ()))
+
+
+def attend_block(q, do, k_cat, v_cat, kt_cat, vt_cat, factor):
+    f32 = jnp.float32
+    s = lax.dot_general(k_cat, q, NT, preferred_element_type=f32)
+    dp = lax.dot_general(v_cat, do, NT, preferred_element_type=f32)
+    top = jnp.max(s, axis=0, keepdims=True)
+    e = jnp.exp((s - top) * factor)
+    inv = 1.0 / jnp.sum(e, axis=0, keepdims=True)
+    p = e * inv
+    delta = jnp.sum(p * dp, axis=0, keepdims=True)
+    pb = p.astype(jnp.bfloat16)
+    ds = (p * (dp - delta)).astype(jnp.bfloat16)
+    attn_t = jnp.dot(vt_cat, pb, preferred_element_type=f32)
+    dq_t = jnp.dot(kt_cat, ds, preferred_element_type=f32) * factor
+    dv = jnp.dot(pb, do, preferred_element_type=f32)
+    dk = jnp.dot(ds, q, preferred_element_type=f32)
+    return attn_t.T.astype(jnp.bfloat16), dq_t.T.astype(jnp.bfloat16), dk, dv
+
+
+def attend_kernel(unroll, spans_n, factor, ids_ref, q_ref, do_ref, k_ref, v_ref, at_ref, dq_ref, dk_ref, dv_ref, kt, vt, dka, dva):
+    step = pl.program_id(0)
+    docs = k_ref.shape[0]
+
+    @pl.when(step == 0)
+    def _():
+        dka[...] = jnp.zeros_like(dka)
+        dva[...] = jnp.zeros_like(dva)
+        for d in range(docs):
+            kt[d] = k_ref[d].T
+            vt[d] = v_ref[d].T
+
+    outs = []
+    for u in range(unroll):
+        ids = [ids_ref[step * unroll + u, j] for j in range(spans_n)]
+        q, do = q_ref[u], do_ref[u]
+        k_cat = jnp.concatenate([k_ref[i] for i in ids], axis=0)
+        v_cat = jnp.concatenate([v_ref[i] for i in ids], axis=0)
+        kt_cat = jnp.concatenate([kt[i] for i in ids], axis=1)
+        vt_cat = jnp.concatenate([vt[i] for i in ids], axis=1)
+        outs.append((ids, attend_block(q, do, k_cat, v_cat, kt_cat, vt_cat, factor)))
+    for u, (ids, (at, dq, dk, dv)) in enumerate(outs):
+        at_ref[u] = at
+        dq_ref[u] = dq
+        for j, i in enumerate(ids):
+            dka[i] += dk[j * 128:(j + 1) * 128]
+            dva[i] += dv[j * 128:(j + 1) * 128]
+
+    @pl.when(step == pl.num_programs(0) - 1)
+    def _():
+        dk_ref[...] = (dka[...] * factor).astype(jnp.bfloat16)
+        dv_ref[...] = dva[...].astype(jnp.bfloat16)
+
+
+def attend(ids, q, do, k, v, unroll=2):
+    blocks, rows, width = q.shape
+    docs = k.shape[0]
+    factor = 1.0 / math.sqrt(width)
+    per = pl.BlockSpec((unroll, rows, width), lambda c, ids: (c, 0, 0))
+    whole = pl.BlockSpec((docs, rows, width), lambda c, ids: (0, 0, 0))
+    return pl.pallas_call(
+        functools.partial(attend_kernel, unroll, ids.shape[1], factor),
+        out_shape=[jax.ShapeDtypeStruct(q.shape, q.dtype)] * 2 + [jax.ShapeDtypeStruct(k.shape, k.dtype)] * 2,
+        grid_spec=pltpu.PrefetchScalarGridSpec(
+            num_scalar_prefetch=1, grid=(blocks // unroll,),
+            in_specs=[per, per, whole, whole], out_specs=[per, per, whole, whole],
+            scratch_shapes=[pltpu.VMEM(k.shape, k.dtype)] * 2 + [pltpu.VMEM(k.shape, jnp.float32)] * 2),
+        compiler_params=pltpu.CompilerParams(dimension_semantics=("arbitrary",), vmem_limit_bytes=60 << 20),
+        name="attend",
+    )(ids, q, do, k, v)
 
 def head_pass(q_head, dout_head, key_head, value_head, id_groups):
     factor = 1.0 / math.sqrt(HEAD_DIM)
@@ -108,7 +181,7 @@
     return shaped.reshape(doc_rows, heads_count * HEAD_DIM)
 
 
-def body(query, key, value, d_out, seg_map, spans):
+def body_shared(query, key, value, d_out, seg_map, spans):
     dummy_carry = jnp.zeros((), jnp.int32)
     heads_here = HEADS // lax.axis_size("blk")
     q_rows, dout_rows = (
@@ -179,6 +252,38 @@
     return (attn_out, d_query, key_total.astype(jnp.bfloat16), value_total.astype(jnp.bfloat16))
 
 
+def body(query, key, value, d_out, seg_map, spans):
+    both = ("blk", "head")
+    blks, columns = lax.axis_size("blk"), lax.axis_size("head")
+    ids = spans[seg_map].astype(jnp.int32)
+
+    def cad_out(array):
+        split = array.reshape(array.shape[0], columns, blks, HEAD_DIM).transpose(2, 1, 0, 3)
+        split = split.reshape(blks * columns, array.shape[0], HEAD_DIM)
+        return lax.all_to_all(split, both, split_axis=0, concat_axis=0, tiled=True)
+
+    def cad_back(array):
+        back = lax.all_to_all(array, both, split_axis=0, concat_axis=0, tiled=True)
+        back = back.reshape(blks, columns, array.shape[1], HEAD_DIM).transpose(2, 1, 0, 3)
+        return back.reshape(array.shape[1], HEADS * HEAD_DIM)
+
+    def doc_out(array):
+        split = array.reshape(array.shape[0], blks, HEAD_DIM).transpose(1, 0, 2)
+        return lax.all_to_all(split, "blk", split_axis=0, concat_axis=0, tiled=True)
+
+    def doc_back(array):
+        back = lax.all_to_all(array, "blk", split_axis=0, concat_axis=0, tiled=True)
+        return back.transpose(1, 0, 2).reshape(array.shape[1], blks * HEAD_DIM)
+
+    q, do, k, v = cad_out(query), cad_out(d_out), doc_out(key), doc_out(value)
+    at, dq, dk, dv = attend(ids, q, do, k, v)
+    return cad_back(at), cad_back(dq), doc_back(dk), doc_back(dv)
+
+
+def one_head_each(mesh):
+    return mesh.shape["blk"] * mesh.shape["head"] == HEADS
+
+
 def solution(mesh):
     placed = (
         P(("blk", "head"), None),
@@ -189,7 +294,7 @@
         P(),
     )
     return jax.shard_map(
-        body,
+        body if one_head_each(mesh) else body_shared,
         mesh=mesh,
         in_specs=placed,
         out_specs=(

time: 565 us -> 242 us (0.43)
  matrix products: 137 us -> 0 us
  local copies, waits for them, and re-layouts: 144 us -> 19.6 us
  waiting for transfers between devices: 176 us -> 96.3 us
  blocking collectives: 0 us -> 66.6 us
  Pallas kernels: 0 us -> 35.1 us
  other arithmetic: 34.6 us -> 0.01 us
  starting transfers between devices: 53.1 us -> 23 us
  between operations: 14.1 us -> 0.81 us
    dot_general x56 -> x0, matrix products: 113 us -> none  [the longest x8 22.6 us: one_group(): jnp.dot(one_hot, key_slots.reshape(group_width * SPANS, BLOCK * HEAD_DIM)...]
    all_to_all x0 -> x3, blocking collectives: none -> 66.6 us  [the longest x2 36.6 us: doc_back(): back = lax.all_to_all(array, 'blk', split_axis=0, concat_axis=0, tiled=True)]
    all_gather x2 -> x0, waiting for transfers between devices: 47.5 us -> none  [the longest x1 24.2 us: body(): lax.all_gather(value, 'head', axis=1, tiled=True)]
    pallas_call x0 -> x1, Pallas kernels: none -> 35.1 us  [attend(): pl.pallas_call(functools.partial(attend_kernel, unroll, ids.shape[1], fac...]
    reshape x17 -> x5, local copies, waits for them, and re-layouts: 38 us -> 7.05 us  [the longest x2 2.76 us: cad_out(): array.reshape(array.shape[0], columns, blks, HEAD_DIM).transpose(2, 1, 0, 3)]
    all_to_all x8 -> x5, waiting for transfers between devices: 126 us -> 96.3 us  [the longest x2 49.6 us: cad_out(): return lax.all_to_all(split, both, split_axis=0, concat_axis=0, tiled=True)]
    all_to_all x8 -> x5, starting transfers between devices: 52.8 us -> 23 us  [the longest x2 11.7 us: doc_out(): return lax.all_to_all(split, 'blk', split_axis=0, concat_axis=0, tiled=True)]
    gather x16 -> x1, local copies, waits for them, and re-layouts: 28.6 us -> 1.16 us  [body(): ids = spans[seg_map].astype(jnp.int32)]
  transfers between devices with their start and end apart: 12 -> 5, of which waited for: 8 -> 5; matrix products, arithmetic and copies ran while one was open for 3% -> 4% of each run, Pallas kernels for 0% -> 0%
where the time goes in v1:
time: 242 us; the launch traced here: 241 us
  waiting for transfers between devices  96.3 us (40%)
  blocking collectives  66.6 us (28%)
  Pallas kernels  35.1 us (15%)
  starting transfers between devices  23 us (10%)
  local copies, waits for them, and re-layouts  19.6 us (8%)
    all_to_all x2, waiting for transfers between devices, cad_out(): return lax.all_to_all(split, both, split_axis=0, concat_axis=0, tiled=True)  49.6 us
    all_to_all x2, blocking collectives, doc_back(): back = lax.all_to_all(array, 'blk', split_axis=0, concat_axis=0, tiled=True)  36.6 us
    pallas_call x1, Pallas kernels, attend(): pl.pallas_call(functools.partial(attend_kernel, unroll, ids.shape[1], fac...  35.1 us
    all_to_all x1, blocking collectives, cad_back(): back = lax.all_to_all(array, both, split_axis=0, concat_axis=0, tiled=True)  30.1 us
    all_to_all x2, waiting for transfers between devices, doc_out(): return lax.all_to_all(split, 'blk', split_axis=0, concat_axis=0, tiled=True)  25.6 us
    all_to_all x1, waiting for transfers between devices, cad_back(): back = lax.all_to_all(array, both, split_axis=0, concat_axis=0, tiled=True)  21.1 us
    all_to_all x2, starting transfers between devices, doc_out(): return lax.all_to_all(split, 'blk', split_axis=0, concat_axis=0, tiled=True)  11.7 us
    unnamed x26, local copies, waits for them, and re-layouts  8.7 us
  transfers between devices with their start and end apart: 5, of which 5 were waited for; matrix products, arithmetic and copies ran while one was open for 4% of the time, Pallas kernels for 0%

profile of v1, /device:TPU:0, one launch (start us, length us, event | category | flops | bytes accessed | tf_op | source)
XLA Modules:
  0.0 241.4 jit_solution(11698803389046464422)
XLA Ops:
  0.6 0.0 copy-start
  0.6 1.3 copy.16
  2.0 1.0 copy.17
  3.0 0.0 copy-start.8
  3.0 7.5 %all-to-all-start.2 = ((bf16[16,128,128]{2,1,0:T(8,128)(2,1)}), bf16[16,128,128]{2,1,0:T(8,128)(2,1)S(1)}, u32[]{:S(2)}, u32[]{:S(2)}) async-start(bf16[16,128,128]{2,1,0:T(8,128)(2,1)} %bitcast.5), calls=%async_computation.2 | async-start | bytes 1048576 | tf_op jit(solution)/shard_map/all_to_all | solution.py:272
  10.5 0.0 copy-done.8
  10.5 0.3 copy.18
  10.8 0.0 copy-start.5
  10.8 1.0 copy.19
  11.9 12.9 %all-to-all-done.2.k_ref = bf16[16,128,128]{2,1,0:T(8,128)(2,1)S(1)} async-done(((bf16[16,128,128]{2,1,0:T(8,128)(2,1)}), bf16[16,128,128]{2,1,0:T(8,128)(2,1)S(1)}, u32[]{:S(2)}, u32[]{:S(2)}) %all-to-all-start.2) | async-done | bytes 524320 | tf_op jit(solution)/shard_map/all_to_all | solution.py:272
  24.8 0.0 copy-start.3
  24.8 0.8 copy-done.3
  25.6 4.2 %all-to-all-start.3 = ((bf16[16,128,128]{2,1,0:T(8,128)(2,1)}), bf16[16,128,128]{2,1,0:T(8,128)(2,1)S(1)}, u32[]{:S(2)}, u32[]{:S(2)}) async-start(bf16[16,128,128]{2,1,0:T(8,128)(2,1)} %bitcast.7), calls=%async_computation.3 | async-start | bytes 1048576 | tf_op jit(solution)/shard_map/all_to_all | solution.py:272
  29.8 0.0 copy-done.5
  29.8 0.2 copy.26
  30.0 1.4 copy.14
  31.4 12.6 %all-to-all-done.3.v_ref = bf16[16,128,128]{2,1,0:T(8,128)(2,1)S(1)} async-done(((bf16[16,128,128]{2,1,0:T(8,128)(2,1)}), bf16[16,128,128]{2,1,0:T(8,128)(2,1)S(1)}, u32[]{:S(2)}, u32[]{:S(2)}) %all-to-all-start.3) | async-done | bytes 524320 | tf_op jit(solution)/shard_map/all_to_all | solution.py:272
  44.0 0.0 copy-start.4
  44.0 0.0 copy-start.6
  44.0 0.8 copy-done.4
  44.8 4.1 %all-to-all-start = ((bf16[32,128,128]{2,1,0:T(8,128)(2,1)}), bf16[32,128,128]{2,1,0:T(8,128)(2,1)S(1)}, u32[]{:S(2)}, u32[]{:S(2)}) async-start(bf16[32,128,128]{2,1,0:T(8,128)(2,1)} %bitcast.1), calls=%async_computation | async-start | bytes 2097152 | tf_op jit(solution)/shard_map/all_to_all | solution.py:263
  48.9 0.0 copy-done.6
  48.9 0.2 copy.27
  49.2 1.4 copy.15
  50.6 24.6 %all-to-all-done.q_ref = bf16[32,128,128]{2,1,0:T(8,128)(2,1)S(1)} async-done(((bf16[32,128,128]{2,1,0:T(8,128)(2,1)}), bf16[32,128,128]{2,1,0:T(8,128)(2,1)S(1)}, u32[]{:S(2)}, u32[]{:S(2)}) %all-to-all-start) | async-done | bytes 1048608 | tf_op jit(solution)/shard_map/all_to_all | solution.py:263
  75.1 0.0 copy-start.1
  75.1 0.0 copy-start.9
  75.1 1.0 copy-done.1
  76.1 3.6 %all-to-all-start.1 = ((bf16[32,128,128]{2,1,0:T(8,128)(2,1)}), bf16[32,128,128]{2,1,0:T(8,128)(2,1)S(1)}, u32[]{:S(2)}, u32[]{:S(2)}) async-start(bf16[32,128,128]{2,1,0:T(8,128)(2,1)} %bitcast.3), calls=%async_computation.1 | async-start | bytes 2097152 | tf_op jit(solution)/shard_map/all_to_all | solution.py:263
  79.7 0.0 copy-done.9
  79.8 0.0 copy-done
  79.8 1.2 gather_fusion
  80.9 25.0 %all-to-all-done.1.do_ref = bf16[32,128,128]{2,1,0:T(8,128)(2,1)S(1)} async-done(((bf16[32,128,128]{2,1,0:T(8,128)(2,1)}), bf16[32,128,128]{2,1,0:T(8,128)(2,1)S(1)}, u32[]{:S(2)}, u32[]{:S(2)}) %all-to-all-start.1) | async-done | bytes 1048608 | tf_op jit(solution)/shard_map/all_to_all | solution.py:263
  105.9 0.0 copy-start.2
  105.9 1.0 copy-done.2
  106.9 35.1 %attend.1 = (bf16[32,128,128]{2,1,0:T(8,128)(2,1)}, bf16[32,128,128]{2,1,0:T(8,128)(2,1)}, bf16[16,128,128]{2,1,0:T(8,128)(2,1)}, bf16[16,128,128]{2,1,0:T(8,128)(2,1)}) custom-call(s32[32,8]{1,0:T(8,128)} %gather_fusion, bf16[32,128,128]{2,1,0:T(8,128)(2,1)} %copy-done.1, bf16[32,128,128]{2,1,0:T(8,128)(2,1)} %copy-done.2, bf16[16,128,128]{2,1,0:T(8,128)(2,1)} %copy-done.3, ...), custom_call_target="tpu_custom_call" | custom-call | tf_op jit(solution)/shard_map/attend/pallas_call | solution.py:76
  142.0 0.0 copy-start.7
  142.0 18.1 %all_to_all.40 = bf16[16,128,128]{2,1,0:T(8,128)(2,1)S(1)} all-to-all(bf16[16,128,128]{2,1,0:T(8,128)(2,1)} %get-tuple-element.10), channel_id=1, replica_groups=mesh['blk'=16,'head'=2] {'blk'}, dimensions={0} | all-to-all | bytes 1048576 | tf_op jit(solution)/shard_map/all_to_all | solution.py:275
  160.1 18.4 %all_to_all.41 = bf16[16,128,128]{2,1,0:T(8,128)(2,1)S(1)} all-to-all(bf16[16,128,128]{2,1,0:T(8,128)(2,1)} %get-tuple-element.11), channel_id=1, replica_groups=mesh['blk'=16,'head'=2] {'blk'}, dimensions={0} | all-to-all | bytes 1048576 | tf_op jit(solution)/shard_map/all_to_all | solution.py:275
  178.6 0.0 copy-done.7
  178.6 30.1 %all_to_all.42 = bf16[32,128,128]{2,1,0:T(8,128)(2,1)S(1)} all-to-all(bf16[32,128,128]{2,1,0:T(8,128)(2,1)S(1)} %copy-done.7), channel_id=1, replica_groups=mesh['blk'=16,'head'=2] {'blk','head'}, dimensions={0} | all-to-all | bytes 2097152 | tf_op jit(solution)/shard_map/all_to_all | solution.py:266
  208.6 3.6 %all-to-all-start.5 = ((bf16[32,128,128]{2,1,0:T(8,128)(2,1)}), bf16[32,128,128]{2,1,0:T(8,128)(2,1)S(1)}, u32[]{:S(2)}, u32[]{:S(2)}) async-start(bf16[32,128,128]{2,1,0:T(8,128)(2,1)} %get-tuple-element.9), calls=%async_computation.5 | async-start | bytes 2097152 | tf_op jit(solution)/shard_map/all_to_all | solution.py:266
  212.2 1.0 copy.22
  213.3 2.0 copy.24
  215.3 0.3 copy.23
  215.6 1.0 copy.25
  216.6 0.7 copy.20
  217.3 21.1 %all-to-all-done.5 = bf16[32,128,128]{2,1,0:T(8,128)(2,1)S(1)} async-done(((bf16[32,128,128]{2,1,0:T(8,128)(2,1)}), bf16[32,128,128]{2,1,0:T(8,128)(2,1)S(1)}, u32[]{:S(2)}, u32[]{:S(2)}) %all-to-all-start.5) | async-done | bytes 1048608 | tf_op jit(solution)/shard_map/all_to_all | solution.py:266
  238.4 0.7 copy.21
  239.1 2.2 copy_bitcast_fusion
  (2 shorter events, 0.0 us)
Async XLA Ops:
  0.6 79.1 %copy-start = (s32[8,8]{1,0:T(8,128)S(1)}, s32[8,8]{1,0:T(8,128)}, u32[]{:S(2)}) copy-start(s32[8,8]{1,0:T(8,128)} %param.11) | copy-start | bytes 772
  3.0 7.5 %copy-start.8 = (bf16[128,2048]{1,0:T(8,128)(2,1)S(1)}, bf16[128,2048]{1,0:T(8,128)(2,1)}, u32[]{:S(2)}) copy-start(bf16[128,2048]{1,0:T(8,128)(2,1)} %param.8) | copy-start | bytes 1572868
  3.0 21.8 %all-to-all-start.2 = ((bf16[16,128,128]{2,1,0:T(8,128)(2,1)}), bf16[16,128,128]{2,1,0:T(8,128)(2,1)S(1)}, u32[]{:S(2)}, u32[]{:S(2)}) async-start(bf16[16,128,128]{2,1,0:T(8,128)(2,1)} %bitcast.5), calls=%async_computation.2 | async-start | bytes 1048576 | tf_op jit(solution)/shard_map/all_to_all | solution.py:272
  10.8 18.9 %copy-start.5 = (bf16[128,4096]{1,0:T(8,128)(2,1)S(1)}, bf16[128,4096]{1,0:T(8,128)(2,1)}, u32[]{:S(2)}) copy-start(bf16[128,4096]{1,0:T(8,128)(2,1)} %param.6) | copy-start | bytes 3145732
  24.8 0.8 copy-start.3
  25.6 18.4 %all-to-all-start.3 = ((bf16[16,128,128]{2,1,0:T(8,128)(2,1)}), bf16[16,128,128]{2,1,0:T(8,128)(2,1)S(1)}, u32[]{:S(2)}, u32[]{:S(2)}) async-start(bf16[16,128,128]{2,1,0:T(8,128)(2,1)} %bitcast.7), calls=%async_computation.3 | async-start | bytes 1048576 | tf_op jit(solution)/shard_map/all_to_all | solution.py:272
  44.0 0.8 copy-start.4
  44.0 4.9 %copy-start.6 = (bf16[128,4096]{1,0:T(8,128)(2,1)S(1)}, bf16[128,4096]{1,0:T(8,128)(2,1)}, u32[]{:S(2)}) copy-start(bf16[128,4096]{1,0:T(8,128)(2,1)} %param.9) | copy-start | bytes 3145732
  44.8 30.3 %all-to-all-start = ((bf16[32,128,128]{2,1,0:T(8,128)(2,1)}), bf16[32,128,128]{2,1,0:T(8,128)(2,1)S(1)}, u32[]{:S(2)}, u32[]{:S(2)}) async-start(bf16[32,128,128]{2,1,0:T(8,128)(2,1)} %bitcast.1), calls=%async_computation | async-start | bytes 2097152 | tf_op jit(solution)/shard_map/all_to_all | solution.py:263
  75.1 1.0 copy-start.1
  75.1 4.6 %copy-start.9 = (s32[32]{0:T(128)S(1)}, s32[32]{0:T(128)}, u32[]{:S(2)}) copy-start(s32[32]{0:T(128)} %param.10) | copy-start | bytes 388
  76.1 29.8 %all-to-all-start.1 = ((bf16[32,128,128]{2,1,0:T(8,128)(2,1)}), bf16[32,128,128]{2,1,0:T(8,128)(2,1)S(1)}, u32[]{:S(2)}, u32[]{:S(2)}) async-start(bf16[32,128,128]{2,1,0:T(8,128)(2,1)} %bitcast.3), calls=%async_computation.1 | async-start | bytes 2097152 | tf_op jit(solution)/shard_map/all_to_all | solution.py:263
  105.9 1.0 copy-start.2
  142.0 36.6 %copy-start.7 = (bf16[32,128,128]{2,1,0:T(8,128)(2,1)S(1)}, bf16[32,128,128]{2,1,0:T(8,128)(2,1)}, u32[]{:S(2)}) copy-start(bf16[32,128,128]{2,1,0:T(8,128)(2,1)} %get-tuple-element.8) | copy-start | bytes 3145732
  208.6 29.8 %all-to-all-start.5 = ((bf16[32,128,128]{2,1,0:T(8,128)(2,1)}), bf16[32,128,128]{2,1,0:T(8,128)(2,1)S(1)}, u32[]{:S(2)}, u32[]{:S(2)}) async-start(bf16[32,128,128]{2,1,0:T(8,128)(2,1)} %get-tuple-element.9), calls=%async_computation.5 | async-start | bytes 2097152 | tf_op jit(solution)/shard_map/all_to_all | solution.py:266

commit v2 on v0

--- a/solution.py
+++ b/solution.py
@@ -1,14 +1,244 @@
+import functools
 import math
 
 import jax
 import jax.numpy as jnp
 from jax import lax
+from jax.experimental import pallas as pl
+from jax.experimental.pallas import tpu as pltpu
 from jax.sharding import PartitionSpec as P
 
 HEADS = 32
 HEAD_DIM = 128
 BLOCK = 128
 SPANS = 8
+
+NT = (((1,), (1,)), ((), ()))
+MESH = pl.DeviceIdType.MESH
+
+
+def attend_block(q, do, k_cat, v_cat, kt_cat, vt_cat, factor):
+    f32 = jnp.float32
+    s = lax.dot_general(k_cat, q, NT, preferred_element_type=f32)
+    dp = lax.dot_general(v_cat, do, NT, preferred_element_type=f32)
+    top = jnp.max(s, axis=0, keepdims=True)
+    e = jnp.exp((s - top) * factor)
+    inv = 1.0 / jnp.sum(e, axis=0, keepdims=True)
+    p = e * inv
+    delta = jnp.sum(p * dp, axis=0, keepdims=True)
+    pb = p.astype(jnp.bfloat16)
+    ds = (p * (dp - delta)).astype(jnp.bfloat16)
+    attn_t = jnp.dot(vt_cat, pb, preferred_element_type=f32)
+    dq_t = jnp.dot(kt_cat, ds, preferred_element_type=f32) * factor
+    return attn_t.T.astype(jnp.bfloat16), dq_t.T.astype(jnp.bfloat16), pb, ds
+
+
+def fused_kernel(
+    blks, columns, unroll, factor,
+    ids_ref, slot_ref, q_in, do_in, k_in, v_in,
+    at_out, dq_out, dk_out, dv_out,
+    q_s, do_s, k_s, v_s, kt, vt, p_s, ds_s, at_s, dq_s, dk_s, dv_s,
+    in_send, out_send, kv_recv, q_recv, do_recv, out_recv,
+):
+    count = blks * columns
+    docs = k_s.shape[0]
+    per_blk = docs // blks
+    blk, col = lax.axis_index("blk"), lax.axis_index("head")
+    me = blk * columns + col
+    my_head = col * blks + blk
+
+    def cols(index):
+        return pl.ds(pl.multiple_of(index * HEAD_DIM, HEAD_DIM), HEAD_DIM)
+
+    def place(t):
+        to = lax.rem(me + t, count)
+        return to // columns, lax.rem(to, columns)
+
+    def remote(src, dst, send, recv, where):
+        pltpu.make_async_remote_copy(
+            src_ref=src, dst_ref=dst, send_sem=send, recv_sem=recv,
+            device_id=where, device_id_type=MESH,
+        ).start()
+
+    barrier = pltpu.get_barrier_semaphore()
+
+    @pl.loop(1, count)
+    def _(t):
+        pl.semaphore_signal(barrier, inc=1, device_id=place(t), device_id_type=MESH)
+
+    pltpu.make_async_copy(k_in.at[:, cols(blk)], k_s.at[blk], kv_recv.at[0]).start()
+    pltpu.make_async_copy(v_in.at[:, cols(blk)], v_s.at[blk], kv_recv.at[1]).start()
+    pltpu.make_async_copy(q_in.at[:, cols(my_head)], q_s.at[me], q_recv.at[me]).start()
+    pltpu.make_async_copy(do_in.at[:, cols(my_head)], do_s.at[me], do_recv.at[me]).start()
+    pl.semaphore_wait(barrier, count - 1)
+
+    @pl.loop(1, blks)
+    def _(t):
+        to = lax.rem(blk + t, blks)
+        remote(k_in.at[:, cols(to)], k_s.at[blk], in_send.at[0], kv_recv.at[0], (to, col))
+        remote(v_in.at[:, cols(to)], v_s.at[blk], in_send.at[1], kv_recv.at[1], (to, col))
+
+    @pl.loop(1, count)
+    def _(t):
+        b, c = place(t)
+        head = c * blks + b
+        remote(q_in.at[:, cols(head)], q_s.at[me], in_send.at[2], q_recv.at[me], (b, c))
+        remote(do_in.at[:, cols(head)], do_s.at[me], in_send.at[3], do_recv.at[me], (b, c))
+
+    @pl.loop(0, count)
+    def _(c):
+        p_s[c, SPANS] = jnp.zeros((BLOCK, BLOCK), jnp.bfloat16)
+        ds_s[c, SPANS] = jnp.zeros((BLOCK, BLOCK), jnp.bfloat16)
+
+    pltpu.make_async_copy(k_s, k_s, kv_recv.at[0]).wait()
+    pltpu.make_async_copy(v_s, v_s, kv_recv.at[1]).wait()
+    @pl.loop(0, docs)
+    def _(d):
+        kt[d] = k_s[d].T
+        vt[d] = v_s[d].T
+
+    def source(t):
+        return lax.rem(me + count - t, count)
+
+    def send_rows(t):
+        c = source(t)
+        where = (c // columns, lax.rem(c, columns))
+        here = cols(my_head)
+
+        @pl.when(t == 0)
+        def _():
+            pltpu.make_async_copy(at_s.at[c], at_out.at[:, here], out_recv.at[0]).start()
+            pltpu.make_async_copy(dq_s.at[c], dq_out.at[:, here], out_recv.at[1]).start()
+
+        @pl.when(t > 0)
+        def _():
+            remote(at_s.at[c], at_out.at[:, here], out_send.at[0], out_recv.at[0], where)
+            remote(dq_s.at[c], dq_out.at[:, here], out_send.at[1], out_recv.at[1], where)
+
+    @pl.loop(0, count // unroll)
+    def _(step):
+        @pl.when(step > 0)
+        def _():
+            for u in range(unroll):
+                send_rows((step - 1) * unroll + u)
+
+        for u in range(unroll):
+            c = source(step * unroll + u)
+            pltpu.make_async_copy(q_s.at[c], q_s.at[c], q_recv.at[c]).wait()
+            pltpu.make_async_copy(do_s.at[c], do_s.at[c], do_recv.at[c]).wait()
+        results = []
+        for u in range(unroll):
+            c = source(step * unroll + u)
+            ids = [ids_ref[c, j] for j in range(SPANS)]
+            k_cat = jnp.concatenate([k_s[i] for i in ids], axis=0)
+            v_cat = jnp.concatenate([v_s[i] for i in ids], axis=0)
+            kt_cat = jnp.concatenate([kt[i] for i in ids], axis=1)
+            vt_cat = jnp.concatenate([vt[i] for i in ids], axis=1)
+            results.append((c, attend_block(q_s[c], do_s[c], k_cat, v_cat, kt_cat, vt_cat, factor)))
+        for c, (at, dq, pb, ds) in results:
+            at_s[c] = at
+            dq_s[c] = dq
+            p_s[c, 0:SPANS] = pb.reshape(SPANS, BLOCK, BLOCK)
+            ds_s[c, 0:SPANS] = ds.reshape(SPANS, BLOCK, BLOCK)
+
+    for u in range(unroll):
+        send_rows(count - unroll + u)
+
+    def send_doc(t):
+        to = lax.rem(blk + t, blks)
+
+        @pl.when(t == 0)
+        def _():
+            pltpu.make_async_copy(dk_s.at[to], dk_out.at[:, cols(blk)], out_recv.at[2]).start()
+            pltpu.make_async_copy(dv_s.at[to], dv_out.at[:, cols(blk)], out_recv.at[3]).start()
+
+        @pl.when(t > 0)
+        def _():
+            remote(dk_s.at[to], dk_out.at[:, cols(blk)], out_send.at[2], out_recv.at[2], (to, col))
+            remote(dv_s.at[to], dv_out.at[:, cols(blk)], out_send.at[3], out_recv.at[3], (to, col))
+
+    pair, chunk = 2, 8
+
+    @pl.loop(0, docs // pair)
+    def _(step):
+        @pl.when(step > 0)
+        def _():
+            for u in range(pair):
+                send_doc((step - 1) * pair + u)
+
+        to = [lax.rem(blk + step * pair + u, blks) for u in range(pair)]
+        for held, right, out, scale in ((ds_s, q_s, dk_s, factor), (p_s, do_s, dv_s, None)):
+            def part(i, total):
+                left = jnp.concatenate([
+                    jnp.concatenate([held[i * chunk + c, slot_ref[i * chunk + c, d]] for c in range(chunk)], axis=1)
+                    for d in to], axis=0)
+                rows = right[pl.ds(i * chunk, chunk)].reshape(chunk * BLOCK, HEAD_DIM)
+                return total + jnp.dot(left, rows, preferred_element_type=jnp.float32)
+            total = lax.fori_loop(0, count // chunk, part, jnp.zeros((pair * BLOCK, HEAD_DIM), jnp.float32))
+            if scale is not None:
+                total = total * scale
+            for u, d in enumerate(to):
+                out[d] = total[u * BLOCK:(u + 1) * BLOCK].astype(jnp.bfloat16)
+
+    for u in range(pair):
+        send_doc(docs - pair + u)
+
+    def drain(array, blocks, sem):
+        view = array.at[pl.ds(0, blocks)]
+        pltpu.make_async_copy(view, view, sem).wait()
+
+    drain(k_s, blks - 1, in_send.at[0])
+    drain(v_s, blks - 1, in_send.at[1])
+    drain(q_s, count - 1, in_send.at[2])
+    drain(do_s, count - 1, in_send.at[3])
+    drain(at_s, count - 1, out_send.at[0])
+    drain(dq_s, count - 1, out_send.at[1])
+    drain(dk_s, blks - 1, out_send.at[2])
+    drain(dv_s, blks - 1, out_send.at[3])
+    drain(at_s, count, out_recv.at[0])
+    drain(dq_s, count, out_recv.at[1])
+    drain(dk_s, docs, out_recv.at[2])
+    drain(dv_s, docs, out_recv.at[3])
+
+
+def body(query, key, value, d_out, seg_map, spans):
+    blks, columns = lax.axis_size("blk"), lax.axis_size("head")
+    count = blks * columns
+    docs = key.shape[0] // BLOCK * blks
+    ids = spans[seg_map].astype(jnp.int32)
+    match = ids[:, :, None] == jnp.arange(docs, dtype=jnp.int32)
+    place = jnp.arange(SPANS, dtype=jnp.int32)[None, :, None]
+    slot = jnp.min(jnp.where(match, place, SPANS), axis=1)
+    bf16 = jnp.bfloat16
+    rows, tiles = (count, BLOCK, HEAD_DIM), (docs, BLOCK, HEAD_DIM)
+    anywhere = pl.BlockSpec(memory_space=pl.ANY)
+    scalars = pl.BlockSpec(memory_space=pltpu.SMEM)
+    return pl.pallas_call(
+        functools.partial(fused_kernel, blks, columns, 2, 1.0 / math.sqrt(HEAD_DIM)),
+        out_shape=[jax.ShapeDtypeStruct(a.shape, a.dtype) for a in (query, query, key, value)],
+        in_specs=[scalars] * 2 + [anywhere] * 4,
+        out_specs=[anywhere] * 4,
+        scratch_shapes=[
+            pltpu.VMEM(rows, bf16), pltpu.VMEM(rows, bf16),
+            pltpu.VMEM(tiles, bf16), pltpu.VMEM(tiles, bf16),
+            pltpu.VMEM(tiles, bf16), pltpu.VMEM(tiles, bf16),
+            pltpu.VMEM((count, SPANS + 1, BLOCK, BLOCK), bf16),
+            pltpu.VMEM((count, SPANS + 1, BLOCK, BLOCK), bf16),
+            pltpu.VMEM(rows, bf16), pltpu.VMEM(rows, bf16),
+            pltpu.VMEM(tiles, bf16), pltpu.VMEM(tiles, bf16),
+            pltpu.SemaphoreType.DMA((4,)), pltpu.SemaphoreType.DMA((4,)),
+            pltpu.SemaphoreType.DMA((2,)), pltpu.SemaphoreType.DMA((count,)),
+            pltpu.SemaphoreType.DMA((count,)), pltpu.SemaphoreType.DMA((4,)),
+        ],
+        compiler_params=pltpu.CompilerParams(
+            collective_id=0, has_side_effects=True, vmem_limit_bytes=60 << 20
+        ),
+        name="attend",
+    )(ids, slot, query, d_out, key, value)
+
+
+def fits_one_head_each(mesh):
+    return mesh.shape["blk"] * mesh.shape["head"] == HEADS
 
 
 def head_pass(q_head, dout_head, key_head, value_head, id_groups):
@@ -108,7 +338,7 @@
     return shaped.reshape(doc_rows, heads_count * HEAD_DIM)
 
 
-def body(query, key, value, d_out, seg_map, spans):
+def body_shared(query, key, value, d_out, seg_map, spans):
     dummy_carry = jnp.zeros((), jnp.int32)
     heads_here = HEADS // lax.axis_size("blk")
     q_rows, dout_rows = (
@@ -189,7 +419,7 @@
         P(),
     )
     return jax.shard_map(
-        body,
+        body if fits_one_head_each(mesh) else body_shared,
         mesh=mesh,
         in_specs=placed,
         out_specs=(

time: 565 us -> 167 us (0.30)
  the two profiles are of different devices: /device:TPU:0 before, /device:TPU:11 now
where the time goes in v2:
time: 167 us
  Pallas kernels  158 us (95%)
  local copies, waits for them, and re-layouts  7.63 us (5%)
    pallas_call x1, Pallas kernels, body(): pl.pallas_call(functools.partial(fused_kernel, blks, columns, 2, 1.0 / ma...  158 us
    unnamed x14, local copies, waits for them, and re-layouts  6.31 us

profile of v2, /device:TPU:11, one launch (start us, length us, event | category | flops | bytes accessed | tf_op | source)
XLA Modules:
  0.0 166.6 jit_solution(16257924275153765572)
XLA Ops:
  0.6 0.0 copy-start
  0.6 0.7 compare_select_fusion
  1.3 0.0 copy-done
  1.3 0.6 gather_fusion
  1.9 0.0 copy-start.4
  1.9 0.1 copy.10
  2.0 0.5 copy-done.4
  2.5 0.7 copy.11.slot_ref
  3.2 157.6 %attend.1 = (bf16[128,4096]{1,0:T(8,128)(2,1)}, bf16[128,4096]{1,0:T(8,128)(2,1)}, bf16[128,2048]{1,0:T(8,128)(2,1)}, bf16[128,2048]{1,0:T(8,128)(2,1)}) custom-call(s32[32,8]{1,0:T(8,128)} %copy-done.4, s32[32,16]{1,0:T(8,128)} %copy.11.slot_ref, bf16[128,4096]{1,0:T(8,128)(2,1)} %q_in.1, bf16[128,4096]{1,0:T(8,128)(2,1)} %do_in.1, bf16[128,2048]{1,0:T(8,128)(2,1)} %k_in.1, ...), custom_call_target="tpu_custom_call" | custom-call | tf_op jit(solution)/shard_map/attend/pallas_call | solution.py:216
  160.7 0.0 copy-start.1
  160.8 2.4 %copy.16 = bf16[128,4096]{1,0:T(8,128)(2,1)} copy(bf16[128,4096]{1,0:T(8,128)(2,1)} %get-tuple-element.8) | data formatting | bytes 2097152
  163.1 0.0 copy-done.1
  163.1 0.0 copy-start.3
  163.1 1.0 copy.17
  164.1 0.4 copy-done.3
  164.5 0.0 copy-start.2
  164.5 0.8 copy.18
  165.3 0.4 copy-done.2
  165.8 0.8 copy.19
  (2 shorter events, 0.0 us)
Async XLA Ops:
  0.6 0.7 copy-start
  1.9 0.6 copy-start.4
  160.7 2.4 %copy-start.1 = (bf16[128,4096]{1,0:T(8,128)(2,1)S(1)}, bf16[128,4096]{1,0:T(8,128)(2,1)}, u32[]{:S(2)}) copy-start(bf16[128,4096]{1,0:T(8,128)(2,1)} %get-tuple-element.9) | copy-start | bytes 3145732
  163.1 1.4 copy-start.3
  164.5 1.2 copy-start.2

commit v3 on v0

--- a/solution.py
+++ b/solution.py
@@ -1,14 +1,308 @@
+import functools
 import math
 
 import jax
 import jax.numpy as jnp
 from jax import lax
+from jax.experimental import pallas as pl
+from jax.experimental.pallas import tpu as pltpu
 from jax.sharding import PartitionSpec as P
 
 HEADS = 32
 HEAD_DIM = 128
 BLOCK = 128
 SPANS = 8
+
+NT = (((1,), (1,)), ((), ()))
+MESH = pl.DeviceIdType.MESH
+
+
+def attend_block(q, do, k_cat, v_cat, kt_cat, vt_cat, factor):
+    f32 = jnp.float32
+    s = lax.dot_general(k_cat, q, NT, preferred_element_type=f32)
+    dp = lax.dot_general(v_cat, do, NT, preferred_element_type=f32)
+    top = jnp.max(s, axis=0, keepdims=True)
+    e = jnp.exp((s - top) * factor)
+    inv = 1.0 / jnp.sum(e, axis=0, keepdims=True)
+    p = e * inv
+    delta = jnp.sum(p * dp, axis=0, keepdims=True)
+    pb = p.astype(jnp.bfloat16)
+    ds = (p * (dp - delta)).astype(jnp.bfloat16)
+    attn_t = jnp.dot(vt_cat, pb, preferred_element_type=f32)
+    dq_t = jnp.dot(kt_cat, ds, preferred_element_type=f32) * factor
+    return attn_t.T.astype(jnp.bfloat16), dq_t.T.astype(jnp.bfloat16), pb, ds
+
+
+def fused_kernel(
+    blks, columns, parts, unroll, factor,
+    seg_ref, spans_ref, slot_ref, q_in, do_in, k_in, v_in,
+    at_out, dq_out, dk_out, dv_out,
+    q_s, do_s, k_s, v_s, kn, vn, kt, vt, p_s, ds_s, at_s, dq_s, dk_s, dv_s,
+    in_send, out_send, k_recv, v_recv, q_recv, do_recv, out_recv,
+):
+    count = blks * columns
+    near = blks // parts
+    members = near * columns
+    each = HEADS // members
+    docs = blks
+    blk, col = lax.axis_index("blk"), lax.axis_index("head")
+    part, spot = blk // near, lax.rem(blk, near)
+    mine = spot * columns + col
+    bf16 = jnp.bfloat16
+
+    def cols(index):
+        return pl.ds(pl.multiple_of(index * HEAD_DIM, HEAD_DIM), HEAD_DIM)
+
+    def member(m):
+        return part * near + m // columns, lax.rem(m, columns)
+
+    def doc_head(b, h):
+        return lax.rem(b, near) * each + h
+
+    def cad_head(m, h):
+        return lax.rem(m, columns) * (HEADS // columns) + m // columns * each + h
+
+    def local(src, dst, sem):
+        pltpu.make_async_copy(src, dst, sem).start()
+
+    def remote(src, dst, send, recv, where):
+        pltpu.make_async_remote_copy(
+            src_ref=src, dst_ref=dst, send_sem=send, recv_sem=recv,
+            device_id=where, device_id_type=MESH,
+        ).start()
+
+    barrier = pltpu.get_barrier_semaphore()
+
+    @pl.loop(1, count)
+    def _(t):
+        to = lax.rem(blk * columns + col + t, count)
+        where = (to // columns, lax.rem(to, columns))
+        pl.semaphore_signal(barrier, inc=1, device_id=where, device_id_type=MESH)
+
+    for h in range(each):
+        doc, cad = doc_head(blk, h), cad_head(mine, h)
+        local(k_in.at[:, cols(doc)], k_s.at[h * docs + blk], k_recv.at[h])
+        local(v_in.at[:, cols(doc)], v_s.at[h * docs + blk], v_recv.at[h])
+        at = h * members + mine
+        local(q_in.at[:, cols(cad)], q_s.at[at], q_recv.at[at])
+        local(do_in.at[:, cols(cad)], do_s.at[at], do_recv.at[at])
+    pl.semaphore_wait(barrier, count - 1)
+
+    @pl.loop(0, each)
+    def _(h):
+        @pl.loop(1, blks)
+        def _(t):
+            to = lax.rem(blk + t, blks)
+            doc = cols(doc_head(to, h))
+            slot = h * docs + blk
+            remote(k_in.at[:, doc], k_s.at[slot], in_send.at[0], k_recv.at[h], (to, col))
+            remote(v_in.at[:, doc], v_s.at[slot], in_send.at[1], v_recv.at[h], (to, col))
+
+        @pl.loop(1, members)
+        def _(t):
+            m = lax.rem(mine + t, members)
+            cad = cols(cad_head(m, h))
+            slot = h * members + mine
+            remote(q_in.at[:, cad], q_s.at[slot], in_send.at[2], q_recv.at[slot], member(m))
+            remote(do_in.at[:, cad], do_s.at[slot], in_send.at[3], do_recv.at[slot], member(m))
+
+    @pl.loop(0, members)
+    def _(m):
+        p_s[m, SPANS] = jnp.zeros((BLOCK, BLOCK), bf16)
+        ds_s[m, SPANS] = jnp.zeros((BLOCK, BLOCK), bf16)
+
+    def wait_for(view, sem):
+        pltpu.make_async_copy(view, view, sem).wait()
+
+    def source(t):
+        return lax.rem(mine + members - t, members)
+
+    pair, chunk = 2, 8
+
+    @pl.loop(0, each)
+    def _(h):
+        wait_for(k_s.at[pl.ds(h * docs, docs)], k_recv.at[h])
+        wait_for(v_s.at[pl.ds(h * docs, docs)], v_recv.at[h])
+
+        @pl.loop(0, docs)
+        def _(d):
+            k_tile, v_tile = k_s[h * docs + d], v_s[h * docs + d]
+            kn[d] = k_tile
+            vn[d] = v_tile
+            kt[d] = k_tile.T
+            vt[d] = v_tile.T
+
+        here = cols(cad_head(mine, h))
+        there = cols(doc_head(blk, h))
+
+        def send_rows(t):
+            m = source(t)
+            slot = h * members + m
+
+            @pl.when(t == 0)
+            def _():
+                local(at_s.at[slot], at_out.at[:, here], out_recv.at[0])
+                local(dq_s.at[slot], dq_out.at[:, here], out_recv.at[1])
+
+            @pl.when(t > 0)
+            def _():
+                remote(at_s.at[slot], at_out.at[:, here], out_send.at[0], out_recv.at[0], member(m))
+                remote(dq_s.at[slot], dq_out.at[:, here], out_send.at[1], out_recv.at[1], member(m))
+
+        @pl.loop(0, members // unroll)
+        def _(step):
+            @pl.when(step > 0)
+            def _():
+                for u in range(unroll):
+                    send_rows((step - 1) * unroll + u)
+
+            for u in range(unroll):
+                slot = h * members + source(step * unroll + u)
+                wait_for(q_s.at[slot], q_recv.at[slot])
+                wait_for(do_s.at[slot], do_recv.at[slot])
+            results = []
+            for u in range(unroll):
+                m = source(step * unroll + u)
+                slot = h * members + m
+                seg = seg_ref[part * members + m]
+                ids = [spans_ref[seg, j] for j in range(SPANS)]
+                k_cat = jnp.concatenate([kn[i] for i in ids], axis=0)
+                v_cat = jnp.concatenate([vn[i] for i in ids], axis=0)
+                kt_cat = jnp.concatenate([kt[i] for i in ids], axis=1)
+                vt_cat = jnp.concatenate([vt[i] for i in ids], axis=1)
+                q, do = q_s[slot], do_s[slot]
+                results.append((m, slot, attend_block(q, do, k_cat, v_cat, kt_cat, vt_cat, factor)))
+            for m, slot, (at, dq, pb, ds) in results:
+                at_s[slot] = at
+                dq_s[slot] = dq
+                p_s[m, 0:SPANS] = pb.reshape(SPANS, BLOCK, BLOCK)
+                ds_s[m, 0:SPANS] = ds.reshape(SPANS, BLOCK, BLOCK)
+
+        for u in range(unroll):
+            send_rows(members - unroll + u)
+
+        def send_doc(t):
+            to = lax.rem(blk + t, blks)
+            slot = h * docs + to
+            dk_to, dv_to = dk_out.at[part, :, there], dv_out.at[part, :, there]
+
+            @pl.when(t == 0)
+            def _():
+                local(dk_s.at[slot], dk_to, out_recv.at[2])
+                local(dv_s.at[slot], dv_to, out_recv.at[3])
+
+            @pl.when(t > 0)
+            def _():
+                remote(dk_s.at[slot], dk_to, out_send.at[2], out_recv.at[2], (to, col))
+                remote(dv_s.at[slot], dv_to, out_send.at[3], out_recv.at[3], (to, col))
+
+        @pl.loop(0, docs // pair)
+        def _(step):
+            @pl.when(step > 0)
+            def _():
+                for u in range(pair):
+                    send_doc((step - 1) * pair + u)
+
+            to = [lax.rem(blk + step * pair + u, blks) for u in range(pair)]
+            for held, right, out, scale in ((ds_s, q_s, dk_s, factor), (p_s, do_s, dv_s, None)):
+                total = jnp.zeros((pair * BLOCK, HEAD_DIM), jnp.float32)
+                for i in range(0, members, chunk):
+                    segs = [seg_ref[part * members + i + c] for c in range(chunk)]
+                    left = jnp.concatenate([
+                        jnp.concatenate([held[i + c, slot_ref[segs[c], d]] for c in range(chunk)], axis=1)
+                        for d in to], axis=0)
+                    rows = right[pl.ds(h * members + i, chunk)].reshape(chunk * BLOCK, HEAD_DIM)
+                    total = total + jnp.dot(left, rows, preferred_element_type=jnp.float32)
+                if scale is not None:
+                    total = total * scale
+                for u, d in enumerate(to):
+                    out[h * docs + d] = total[u * BLOCK:(u + 1) * BLOCK].astype(bf16)
+
+        for u in range(pair):
+            send_doc(docs - pair + u)
+
+    def drain(array, blocks, sem):
+        wait_for(array.at[pl.ds(0, blocks)], sem)
+
+    for i, array in enumerate((k_s, v_s, q_s, do_s)):
+        drain(array, each * ((blks if i < 2 else members) - 1), in_send.at[i])
+    for i, array in enumerate((at_s, dq_s, dk_s, dv_s)):
+        drain(array, each * ((members if i < 2 else blks) - 1), out_send.at[i])
+    for i, array in enumerate((at_s, dq_s, dk_s, dv_s)):
+        drain(array, each * (members if i < 2 else blks), out_recv.at[i])
+
+
+def finish_kernel(at_in, dq_in, dk_in, dv_in, at_ref, dq_ref, dk_ref, dv_ref):
+    at_ref[...] = at_in[...]
+    dq_ref[...] = dq_in[...]
+    for src, dst in ((dk_in, dk_ref), (dv_in, dv_ref)):
+        total = src[0].astype(jnp.float32)
+        for p in range(1, src.shape[0]):
+            total = total + src[p].astype(jnp.float32)
+        dst[...] = total.astype(jnp.bfloat16)
+
+
+def finish(at, dq, dk, dv, steps=4):
+    rows, wide = at.shape
+    parts, docs, narrow = dk.shape
+    cad = pl.BlockSpec((rows, wide // steps), lambda i: (0, i))
+    partial = pl.BlockSpec((parts, docs, narrow // steps), lambda i: (0, 0, i))
+    doc = pl.BlockSpec((docs, narrow // steps), lambda i: (0, i))
+    return pl.pallas_call(
+        finish_kernel,
+        grid=(steps,),
+        out_shape=[jax.ShapeDtypeStruct(a.shape[-2:], a.dtype) for a in (at, dq, dk, dv)],
+        in_specs=[cad, cad, partial, partial],
+        out_specs=[cad, cad, doc, doc],
+        name="finish",
+    )(at, dq, dk, dv)
+
+
+def body(query, key, value, d_out, seg_map, spans):
+    blks, columns = lax.axis_size("blk"), lax.axis_size("head")
+    parts = 2
+    docs = blks
+    members = blks // parts * columns
+    each = HEADS // members
+    match = spans[:, :, None] == jnp.arange(docs, dtype=jnp.int32)
+    place = jnp.arange(SPANS, dtype=jnp.int32)[None, :, None]
+    slot = jnp.min(jnp.where(match, place, SPANS), axis=1)
+    bf16 = jnp.bfloat16
+    rows, tiles = (each * members, BLOCK, HEAD_DIM), (each * docs, BLOCK, HEAD_DIM)
+    flipped = (docs, HEAD_DIM, BLOCK)
+    held = (members, SPANS + 1, BLOCK, BLOCK)
+    anywhere = pl.BlockSpec(memory_space=pl.ANY)
+    scalars = pl.BlockSpec(memory_space=pltpu.SMEM)
+    partial = jax.ShapeDtypeStruct((parts, *key.shape), bf16)
+    cad = jax.ShapeDtypeStruct(query.shape, bf16)
+    outs = pl.pallas_call(
+        functools.partial(fused_kernel, blks, columns, parts, 2, 1.0 / math.sqrt(HEAD_DIM)),
+        out_shape=[cad, cad, partial, partial],
+        in_specs=[scalars] * 3 + [anywhere] * 4,
+        out_specs=[anywhere] * 4,
+        scratch_shapes=[
+            pltpu.VMEM(rows, bf16), pltpu.VMEM(rows, bf16),
+            pltpu.VMEM(tiles, bf16), pltpu.VMEM(tiles, bf16),
+            pltpu.VMEM((docs, BLOCK, HEAD_DIM), bf16), pltpu.VMEM((docs, BLOCK, HEAD_DIM), bf16),
+            pltpu.VMEM(flipped, bf16), pltpu.VMEM(flipped, bf16),
+            pltpu.VMEM(held, bf16), pltpu.VMEM(held, bf16),
+            pltpu.VMEM(rows, bf16), pltpu.VMEM(rows, bf16),
+            pltpu.VMEM(tiles, bf16), pltpu.VMEM(tiles, bf16),
+            pltpu.SemaphoreType.DMA((4,)), pltpu.SemaphoreType.DMA((4,)),
+            pltpu.SemaphoreType.DMA((each,)), pltpu.SemaphoreType.DMA((each,)),
+            pltpu.SemaphoreType.DMA((each * members,)), pltpu.SemaphoreType.DMA((each * members,)),
+            pltpu.SemaphoreType.DMA((4,)),
+        ],
+        compiler_params=pltpu.CompilerParams(
+            collective_id=0, has_side_effects=True, vmem_limit_bytes=60 << 20
+        ),
+        name="attend",
+    )(seg_map, spans, slot, query, d_out, key, value)
+    return finish(*outs)
+
+
+def fits_one_head_each(mesh):
+    return mesh.shape["blk"] * mesh.shape["head"] == HEADS
 
 
 def head_pass(q_head, dout_head, key_head, value_head, id_groups):
@@ -108,7 +402,7 @@
     return shaped.reshape(doc_rows, heads_count * HEAD_DIM)
 
 
-def body(query, key, value, d_out, seg_map, spans):
+def body_shared(query, key, value, d_out, seg_map, spans):
     dummy_carry = jnp.zeros((), jnp.int32)
     heads_here = HEADS // lax.axis_size("blk")
     q_rows, dout_rows = (
@@ -189,7 +483,7 @@
         P(),
     )
     return jax.shard_map(
-        body,
+        body if fits_one_head_each(mesh) else body_shared,
         mesh=mesh,
         in_specs=placed,
         out_specs=(

time: 565 us -> 133 us (0.24)
  waiting for transfers between devices: 176 us -> 0 us
  local copies, waits for them, and re-layouts: 144 us -> 0 us
  matrix products: 137 us -> 0 us
  Pallas kernels: 0 us -> 131 us
  starting transfers between devices: 53.1 us -> 0 us
  other arithmetic: 34.6 us -> 1.37 us
  between operations: 14.1 us -> 0.64 us
    pallas_call x0 -> x2, Pallas kernels: none -> 131 us  [the longest x1 127 us: body(): pl.pallas_call(functools.partial(fused_kernel, blks, columns, parts, 2, 1...]
    all_to_all x8 -> x0, waiting for transfers between devices: 126 us -> none  [the longest x1 22.5 us: body(): lax.all_to_all(key_wide, 'blk', split_axis=1, concat_axis=0, tiled=True)]
    dot_general x56 -> x0, matrix products: 113 us -> none  [the longest x8 22.6 us: one_group(): jnp.dot(one_hot, key_slots.reshape(group_width * SPANS, BLOCK * HEAD_DIM)...]
    all_to_all x8 -> x0, starting transfers between devices: 52.8 us -> none  [the longest x1 7.44 us: body(): lax.all_to_all(query, 'blk', split_axis=1, concat_axis=0, tiled=True)]
    all_gather x2 -> x0, waiting for transfers between devices: 47.5 us -> none  [the longest x1 24.2 us: body(): lax.all_gather(value, 'head', axis=1, tiled=True)]
    reshape x17 -> x0, local copies, waits for them, and re-layouts: 38 us -> none  [the longest x8 22.8 us: one_group(): key_slots.reshape(group_width * SPANS, BLOCK * HEAD_DIM)]
    gather x16 -> x0, local copies, waits for them, and re-layouts: 28.6 us -> none  [the longest x8 14.3 us: one_group(): jnp.take(value_head, flat_ids, axis=0)]
    sub x8 -> x0, matrix products: 24.1 us -> none  [one_group(): expo = jnp.exp(scores - top_score)]
  transfers between devices with their start and end apart: 12 -> 0, of which waited for: 8 -> 0; matrix products, arithmetic and copies ran while one was open for 3% -> 0% of each run, Pallas kernels for 0% -> 0%
where the time goes in v3:
time: 133 us
  Pallas kernels  131 us (98%)
  other arithmetic  1.37 us (1%)
    pallas_call x1, Pallas kernels, body(): pl.pallas_call(functools.partial(fused_kernel, blks, columns, parts, 2, 1...  127 us
    pallas_call x1, Pallas kernels, finish(): pl.pallas_call(finish_kernel, grid=(steps,), out_shape=[jax.ShapeDtypeStr...  4.32 us

profile of v3, /device:TPU:0, one launch (start us, length us, event | category | flops | bytes accessed | tf_op | source)
XLA Modules:
  0.0 133.2 jit_solution(8461868538609156786)
XLA Ops:
  0.6 1.4 %select_reduce_fusion.slot_ref = s32[8,16]{1,0:T(8,128)} fusion(s32[8,8]{1,0:T(8,128)} %spans_ref.1), kind=kLoop, calls=%fused_computation | loop fusion | flops 2944 | bytes 768 | tf_op jit(solution)/shard_map/reduce_min | solution.py:269
  2.0 126.9 %attend.1 = (bf16[128,4096]{1,0:T(8,128)(2,1)}, bf16[128,4096]{1,0:T(8,128)(2,1)}, bf16[2,128,2048]{2,1,0:T(8,128)(2,1)}, bf16[2,128,2048]{2,1,0:T(8,128)(2,1)}) custom-call(s32[32]{0:T(128)} %seg_ref.1, s32[8,8]{1,0:T(8,128)} %spans_ref.1, s32[8,16]{1,0:T(8,128)} %select_reduce_fusion.slot_ref, bf16[128,4096]{1,0:T(8,128)(2,1)} %q_in.1, ...), custom_call_target="tpu_custom_call" | custom-call | tf_op jit(solution)/shard_map/attend/pallas_call | solution.py:278
  128.9 4.3 %finish.1 = (bf16[128,4096]{1,0:T(8,128)(2,1)}, bf16[128,4096]{1,0:T(8,128)(2,1)}, bf16[128,2048]{1,0:T(8,128)(2,1)}, bf16[128,2048]{1,0:T(8,128)(2,1)}) custom-call(bf16[128,4096]{1,0:T(8,128)(2,1)} %get-tuple-element.8.at_in, bf16[128,4096]{1,0:T(8,128)(2,1)} %get-tuple-element.9.dq_in, bf16[2,128,2048]{2,1,0:T(8,128)(2,1)} %get-tuple-element.10.dk_in, ...), custom_call_target="tpu_custom_call" | custom-call | tf_op jit(solution)/shard_map/finish/pallas_call | solution.py:251

commit v4 on v3

--- a/solution.py
+++ b/solution.py
@@ -35,10 +35,10 @@
 
 def fused_kernel(
     blks, columns, parts, unroll, factor,
-    seg_ref, spans_ref, slot_ref, q_in, do_in, k_in, v_in,
+    seg_ref, spans_ref, q_in, do_in, k_in, v_in,
     at_out, dq_out, dk_out, dv_out,
     q_s, do_s, k_s, v_s, kn, vn, kt, vt, p_s, ds_s, at_s, dq_s, dk_s, dv_s,
-    in_send, out_send, k_recv, v_recv, q_recv, do_recv, out_recv,
+    slot_ref, in_send, out_send, k_recv, v_recv, q_recv, do_recv, out_recv,
 ):
     count = blks * columns
     near = blks // parts
@@ -62,6 +62,11 @@
     def cad_head(m, h):
         return lax.rem(m, columns) * (HEADS // columns) + m // columns * each + h
 
+    def turn(t, size):
+        half = (t + 1) // 2
+        back = lax.rem(t + 1, 2)
+        return lax.rem(half + back * (size - 2 * half) + size, size)
+
     def local(src, dst, sem):
         pltpu.make_async_copy(src, dst, sem).start()
 
@@ -92,7 +97,7 @@
     def _(h):
         @pl.loop(1, blks)
         def _(t):
-            to = lax.rem(blk + t, blks)
+            to = lax.rem(blk + turn(t, blks), blks)
             doc = cols(doc_head(to, h))
             slot = h * docs + blk
             remote(k_in.at[:, doc], k_s.at[slot], in_send.at[0], k_recv.at[h], (to, col))
@@ -100,12 +105,21 @@
 
         @pl.loop(1, members)
         def _(t):
-            m = lax.rem(mine + t, members)
+            m = lax.rem(mine + turn(t, members), members)
             cad = cols(cad_head(m, h))
             slot = h * members + mine
             remote(q_in.at[:, cad], q_s.at[slot], in_send.at[2], q_recv.at[slot], member(m))
             remote(do_in.at[:, cad], do_s.at[slot], in_send.at[3], do_recv.at[slot], member(m))
 
+    @pl.loop(0, spans_ref.shape[0])
+    def _(g):
+        named = [spans_ref[g, j] for j in range(SPANS)]
+        for d in range(docs):
+            found = SPANS
+            for j in range(SPANS):
+                found = jnp.where(named[j] == d, j, found)
+            slot_ref[g, d] = found
+
     @pl.loop(0, members)
     def _(m):
         p_s[m, SPANS] = jnp.zeros((BLOCK, BLOCK), bf16)
@@ -115,7 +129,7 @@
         pltpu.make_async_copy(view, view, sem).wait()
 
     def source(t):
-        return lax.rem(mine + members - t, members)
+        return lax.rem(mine + members - turn(t, members), members)
 
     pair, chunk = 2, 8
 
@@ -182,7 +196,7 @@
             send_rows(members - unroll + u)
 
         def send_doc(t):
-            to = lax.rem(blk + t, blks)
+            to = lax.rem(blk + turn(t, blks), blks)
             slot = h * docs + to
             dk_to, dv_to = dk_out.at[part, :, there], dv_out.at[part, :, there]
 
@@ -203,7 +217,7 @@
                 for u in range(pair):
                     send_doc((step - 1) * pair + u)
 
-            to = [lax.rem(blk + step * pair + u, blks) for u in range(pair)]
+            to = [lax.rem(blk + turn(step * pair + u, blks), blks) for u in range(pair)]
             for held, right, out, scale in ((ds_s, q_s, dk_s, factor), (p_s, do_s, dv_s, None)):
                 total = jnp.zeros((pair * BLOCK, HEAD_DIM), jnp.float32)
                 for i in range(0, members, chunk):
@@ -242,7 +256,7 @@
         dst[...] = total.astype(jnp.bfloat16)
 
 
-def finish(at, dq, dk, dv, steps=4):
+def finish(at, dq, dk, dv, steps=2):
     rows, wide = at.shape
     parts, docs, narrow = dk.shape
     cad = pl.BlockSpec((rows, wide // steps), lambda i: (0, i))
@@ -259,14 +273,13 @@
 
 
 def body(query, key, value, d_out, seg_map, spans):
+    if query.shape[0] != BLOCK or key.shape[0] != BLOCK:
+        return body_shared(query, key, value, d_out, seg_map, spans)
     blks, columns = lax.axis_size("blk"), lax.axis_size("head")
     parts = 2
     docs = blks
     members = blks // parts * columns
     each = HEADS // members
-    match = spans[:, :, None] == jnp.arange(docs, dtype=jnp.int32)
-    place = jnp.arange(SPANS, dtype=jnp.int32)[None, :, None]
-    slot = jnp.min(jnp.where(match, place, SPANS), axis=1)
     bf16 = jnp.bfloat16
     rows, tiles = (each * members, BLOCK, HEAD_DIM), (each * docs, BLOCK, HEAD_DIM)
     flipped = (docs, HEAD_DIM, BLOCK)
@@ -278,7 +291,7 @@
     outs = pl.pallas_call(
         functools.partial(fused_kernel, blks, columns, parts, 2, 1.0 / math.sqrt(HEAD_DIM)),
         out_shape=[cad, cad, partial, partial],
-        in_specs=[scalars] * 3 + [anywhere] * 4,
+        in_specs=[scalars] * 2 + [anywhere] * 4,
         out_specs=[anywhere] * 4,
         scratch_shapes=[
             pltpu.VMEM(rows, bf16), pltpu.VMEM(rows, bf16),
@@ -288,6 +301,7 @@
             pltpu.VMEM(held, bf16), pltpu.VMEM(held, bf16),
             pltpu.VMEM(rows, bf16), pltpu.VMEM(rows, bf16),
             pltpu.VMEM(tiles, bf16), pltpu.VMEM(tiles, bf16),
+            pltpu.SMEM((spans.shape[0], docs), jnp.int32),
             pltpu.SemaphoreType.DMA((4,)), pltpu.SemaphoreType.DMA((4,)),
             pltpu.SemaphoreType.DMA((each,)), pltpu.SemaphoreType.DMA((each,)),
             pltpu.SemaphoreType.DMA((each * members,)), pltpu.SemaphoreType.DMA((each * members,)),
@@ -297,12 +311,12 @@
             collective_id=0, has_side_effects=True, vmem_limit_bytes=60 << 20
         ),
         name="attend",
-    )(seg_map, spans, slot, query, d_out, key, value)
+    )(seg_map, spans, query, d_out, key, value)
     return finish(*outs)
 
 
 def fits_one_head_each(mesh):
-    return mesh.shape["blk"] * mesh.shape["head"] == HEADS
+    return mesh.shape["blk"] * mesh.shape["head"] == HEADS and mesh.shape["blk"] % 8 == 0
 
 
 def head_pass(q_head, dout_head, key_head, value_head, id_groups):

time: 133 us -> 128 us (0.962)
  Pallas kernels: 131 us -> 127 us
  other arithmetic: 1.37 us -> 0 us
    pallas_call x1, Pallas kernels: 127 us -> 124 us  [body(): pl.pallas_call(functools.partial(fused_kernel, blks, columns, parts, 2, 1...]
    reduce_min x1 -> x0, other arithmetic: 1.37 us -> none  [body(): slot = jnp.min(jnp.where(match, place, SPANS), axis=1)]
where the time goes in v4:
time: 128 us
  Pallas kernels  127 us (99%)
    pallas_call x1, Pallas kernels, body(): pl.pallas_call(functools.partial(fused_kernel, blks, columns, parts, 2, 1...  124 us
    pallas_call x1, Pallas kernels, finish(): pl.pallas_call(finish_kernel, grid=(steps,), out_shape=[jax.ShapeDtypeStr...  3.43 us

profile of v4, /device:TPU:0, one launch (start us, length us, event | category | flops | bytes accessed | tf_op | source)
XLA Modules:
  0.0 127.8 jit_solution(794842173105854882)
XLA Ops:
  0.6 123.7 %attend.1 = (bf16[128,4096]{1,0:T(8,128)(2,1)}, bf16[128,4096]{1,0:T(8,128)(2,1)}, bf16[2,128,2048]{2,1,0:T(8,128)(2,1)}, bf16[2,128,2048]{2,1,0:T(8,128)(2,1)}) custom-call(s32[32]{0:T(128)} %seg_ref.1, s32[8,8]{1,0:T(8,128)} %spans_ref.1, bf16[128,4096]{1,0:T(8,128)(2,1)} %q_in.1, bf16[128,4096]{1,0:T(8,128)(2,1)} %do_in.1, bf16[128,2048]{1,0:T(8,128)(2,1)} %k_in.1, ...), custom_call_target="tpu_custom_call" | custom-call | tf_op jit(solution)/shard_map/attend/pallas_call | solution.py:291
  124.4 3.4 %finish.1 = (bf16[128,4096]{1,0:T(8,128)(2,1)}, bf16[128,4096]{1,0:T(8,128)(2,1)}, bf16[128,2048]{1,0:T(8,128)(2,1)}, bf16[128,2048]{1,0:T(8,128)(2,1)}) custom-call(bf16[128,4096]{1,0:T(8,128)(2,1)} %get-tuple-element.8.at_in, bf16[128,4096]{1,0:T(8,128)(2,1)} %get-tuple-element.9.dq_in, bf16[2,128,2048]{2,1,0:T(8,128)(2,1)} %get-tuple-element.10.dk_in, ...), custom_call_target="tpu_custom_call" | custom-call | tf_op jit(solution)/shard_map/finish/pallas_call | solution.py:265
